TPU v7x, 32 devices: a whole 2x2x4 slice. The times are simulated.
32 devices in a mesh: occ: 8 (over y, x, core), ao: 4 (over z).
Axes of the slice: x: 2, y: 2, z: 4, core: 2. Of those that a mesh axis runs over, the one named last changes fastest.
Arguments:
- coef: bfloat16 [2048, 8], P('ao', 'occ'), may hold values from -0.5 to 0.5
- half_ints: bfloat16 [8, 1024, 2048], P('occ', None, 'ao'), may hold values from -0.5 to 0.5
- metric_inv: bfloat16 [64, 128, 128], replicated, may hold values from -1 to 2, as said below
- dom_blocks: int32 [8, 8], P('occ'), may hold values from 0 to 63, as said below
- dom_len: int32 [8], P('occ'), may hold values from 2 to 8
Outputs:
- exchange_k: float32 [2048, 2048], P('ao', 'occ')
- fit_density: float32 [8192], replicated
Inputs may be any that keep to these rules, and one draw needn't show every extreme that they name: `dom_blocks`: each row holds 8 different block numbers. `metric_inv`: full rank blocks.
All inputs are finite; a program needn't handle non-finite values.
Results may differ from a plain program's by a relative error of at most 0.0055.
Values may be sent and summed in bfloat16 or wider, within the bound.
No kernel may reach another device: no remote copies, remote signals or barrier semaphores. Data moves between devices by JAX's collectives and lax.ppermute only.
A program may use at most 128 MiB of HBM per device.

v0:
```python
import jax
import jax.numpy as jnp
from jax import lax
from jax.sharding import PartitionSpec as P


def on_device(coef, half_ints, metric_inv, dom_blocks, dom_len):
    lmo_count, domain, ao_rows = half_ints.shape
    block = metric_inv.shape[1]
    slots = domain // block
    fit_blocks = metric_inv.shape[0]
    metric_rows = metric_inv[dom_blocks]
    raw_ints = half_ints.reshape(lmo_count, slots, block, ao_rows)
    fitted = jnp.einsum(
        "isab,isbm->isam", metric_rows, raw_ints, preferred_element_type=jnp.float32
    )
    live_slots = jnp.arange(slots, dtype=jnp.int32)[None, :] < dom_len[:, None]
    fitted = jnp.where(live_slots[:, :, None, None], fitted, 0.0)
    fitted = fitted.reshape(lmo_count, domain, ao_rows).astype(jnp.bfloat16)
    pair_part = jnp.einsum("ipm,mi->ip", fitted, coef, preferred_element_type=jnp.float32)
    one_hot = (
        dom_blocks[:, :, None] == jnp.arange(fit_blocks, dtype=jnp.int32)[None, None, :]
    ).astype(jnp.float32)
    local_density = jnp.einsum("isf,isr->fr", one_hot, pair_part.reshape(lmo_count, slots, block))
    density = lax.psum(local_density, ("occ", "ao"))
    density = density.reshape(fit_blocks * block)
    partial_value = jnp.einsum(
        "ipm,ipn->mn",
        fitted,
        lax.all_gather(fitted, "ao", axis=2, tiled=True),
        preferred_element_type=jnp.float32,
    )
    exchange_k = lax.psum_scatter(partial_value, "occ", scatter_dimension=1, tiled=True)
    return (exchange_k, density)


def solution(mesh):
    in_specs = (P("ao", "occ"), P("occ", None, "ao"), P(), P("occ", None), P("occ"))
    out_specs = (P("ao", "occ"), P())
    return jax.shard_map(
        on_device, mesh=mesh, in_specs=in_specs, out_specs=out_specs, check_vma=False
    )
```

profile of v0, /device:TPU:0, one launch (start us, length us, event | category | flops | bytes accessed | tf_op | source)
XLA Modules:
  0.0 159.3 jit_solution(12443113816982479165)
XLA Ops:
  7.2 0.0 copy-start
  7.2 0.0 all-gather.2.cloned.1.call-start
  8.0 0.7 fusion.5
  8.7 0.1 copy-done
  8.8 0.6 gather_fusion
  9.4 2.7 %select_convert_fusion = bf16[8,128,512]{2,1,0:T(8,128)(2,1)} fusion(bf16[8,128,128]{2,1,0:T(8,128)(2,1)S(1)} %gather_fusion, bf16[8,128,512]{2,1,0:T(8,128)(2,1)} %bitcast.25, pred[8]{0:T(512)(128)(4,1)S(1)} %iota_compare_fusion.2), kind=kOutput, calls=%fused_computation.3 | convolution fusion | flops 135266304 | bytes 2359304 | tf_op jit(solution)/shard_map/isab,isbm->isam/dot_general | solution.py:14
  12.1 0.0 all-gather.2.cloned.1.call-update
  12.1 0.0 reduce-scatter.2.cloned.1.call-start
  12.1 83.6 %all-gather.2.cloned.1.call-done = bf16[1,1024,2048]{2,1,0:T(8,128)(2,1)} async-done(((bf16[1,1024,512]{2,1,0:T(8,128)(2,1)}), bf16[1,1024,2048]{2,1,0:T(8,128)(2,1)}) %all-gather.2.cloned.1.call-update) | async-done | bytes 4194320 | tf_op jit(solution)/shard_map/all_gather | solution.py:30
  95.7 6.8 %fusion = f32[512,2048]{1,0:T(8,128)} fusion(bf16[1024,512]{1,0:T(8,128)(2,1)} %bitcast.24, bf16[1,1024,2048]{2,1,0:T(8,128)(2,1)} %all-gather.2.cloned.1.call-done), kind=kOutput, calls=%fused_computation.1 | convolution fusion | flops 2147483648 | bytes 9437184 | tf_op jit(solution)/shard_map/ipm,ipn->mn/dot_general | solution.py:27
  102.5 0.0 copy-start.1
  102.5 0.0 copy-start.2
  102.5 0.0 copy-start.3
  102.5 0.0 reduce-scatter.2.cloned.1.call-update
  102.6 1.2 copy-done.1
  103.8 0.0 copy-done.2
  103.8 0.4 fusion.2
  104.1 0.0 copy-done.3
  104.1 0.3 convolution_bitcast_fusion
  104.4 39.3 %psum.7 = f32[8192]{0:T(1024)} all-reduce(f32[8192]{0:T(1024)S(1)} %convolution_bitcast_fusion), channel_id=1, replica_groups=mesh['occ'=8,'ao'=4] {'occ','ao'}, use_global_device_ids=true, to_apply=%region_1.2 | all-reduce | flops 8192 | bytes 65536 | tf_op jit(solution)/shard_map/psum | solution.py:25
  143.7 8.8 %reduce-scatter.2.cloned.1.call-done = f32[512,256]{1,0:T(8,128)} async-done(((f32[512,2048]{1,0:T(8,128)}), f32[512,256]{1,0:T(8,128)}) %reduce-scatter.2.cloned.1.call-update) | async-done | bytes 524304 | tf_op jit(solution)/shard_map/reduce_scatter | solution.py:33
  (2 shorter events, 0.0 us)
Async XLA Ops:
  7.2 1.6 %copy-start = (bf16[64,128,128]{2,1,0:T(8,128)(2,1)S(1)}, bf16[64,128,128]{2,1,0:T(8,128)(2,1)}, u32[]{:S(2)}) copy-start(bf16[64,128,128]{2,1,0:T(8,128)(2,1)} %param.7) | copy-start | bytes 6291460
  7.2 88.5 %all-gather.2.cloned.1.call-start = ((), (), s32[]{:S(2)}) async-start(), calls=%async_computation.1 | async-start | bytes 5242880 | tf_op jit(solution)/shard_map/all_gather | solution.py:30
  12.1 140.4 %reduce-scatter.2.cloned.1.call-start = ((), (), s32[]{:S(2)}) async-start(), calls=%async_computation.2 | async-start | bytes 4718592 | tf_op jit(solution)/shard_map/reduce_scatter | solution.py:33
  102.5 1.2 copy-start.1
  102.5 1.2 copy-start.2
  102.5 1.6 copy-start.3
Sparse Core Ops, SparseCore 0:
  12.2 83.4 all-gather.1
  102.7 49.7 reduce-scatter.1
where the time goes:
time: 160 us; the launch traced here: 159 us
  waiting for transfers between devices  92.3 us (58%)
  blocking collectives  39.3 us (25%)
  between operations  14.9 us (9%)
  matrix products  10.2 us (6%)
  local copies, waits for them, and re-layouts  1.89 us (1%)
    all_gather x1, waiting for transfers between devices, on_device(): lax.all_gather(fitted, 'ao', axis=2, tiled=True)  83.6 us
    psum x1, blocking collectives, on_device(): density = lax.psum(local_density, ('occ', 'ao'))  39.3 us
    reduce_scatter x1, waiting for transfers between devices, on_device(): lax.psum_scatter(partial_value, 'occ', scatter_dimension=1, tiled=True)  8.75 us
    dot_general x1, matrix products, on_device(): jnp.einsum('ipm,ipn->mn', fitted, lax.all_gather(fitted, 'ao', axis=2, ti...  6.82 us
  transfers between devices with their start and end apart: 2, of which 2 were waited for; matrix products, arithmetic and copies ran while one was open for 0% of the time, Pallas kernels for 0%

commit v1 on v0

--- a/solution.py
+++ b/solution.py
@@ -1,10 +1,15 @@
 import jax
 import jax.numpy as jnp
 from jax import lax
+from jax.experimental import pallas as pl
+from jax.experimental.pallas import tpu as pltpu
 from jax.sharding import PartitionSpec as P
 
 
-def on_device(coef, half_ints, metric_inv, dom_blocks, dom_len):
+VMEM_LIMIT = 18 * 2**20
+
+
+def general_plan(coef, half_ints, metric_inv, dom_blocks, dom_len):
     lmo_count, domain, ao_rows = half_ints.shape
     block = metric_inv.shape[1]
     slots = domain // block
@@ -34,9 +39,404 @@
     return (exchange_k, density)
 
 
+def line_plan(n_occ, n_ao):
+    chips = n_occ // 2
+
+    def device(chip, core, plane):
+        return (2 * chip + core) * n_ao + plane
+
+    def both_cores(moves, swap=0):
+        return [
+            (device(src[1], core, src[0]), device(dst[1], core ^ swap, dst[0]))
+            for src, dst in moves
+            for core in range(2)
+        ]
+
+    def one_core(moves):
+        return [
+            (device(chip, core, src), device(chip, core, dst))
+            for core, src, dst in moves
+            for chip in range(chips)
+        ]
+
+    middle = (1, 2)
+    spots = [(p, c) for p in range(n_ao) for c in range(chips)]
+
+    def early_owner(p, c):
+        return abs(p - c) <= 1 or (p in middle and c == p ^ 2)
+
+    early_turn = [((p, c), (c, p)) for p, c in spots if abs(p - c) == 1] + [((1, 3), (2, 0)), ((2, 0), (3, 1))]
+    early_straight = [((1, 3), (0, 2)), ((2, 0), (1, 3))]
+    late_turn = [((1, 3), (3, 1)), ((2, 0), (0, 2)), ((1, 2), (3, 0)), ((2, 1), (0, 3))]
+    late_straight = [((1, 2), (0, 3)), ((2, 1), (3, 0))]
+
+    def on_device(coef, half_ints, metric_inv, dom_blocks, dom_len):
+        _, domain, ao_rows = half_ints.shape
+        fit_blocks, block, _ = metric_inv.shape
+        slots = domain // block
+        half = ao_rows // 2
+        bf16, f32 = jnp.bfloat16, jnp.float32
+        plane = lax.axis_index("ao")
+        occ = lax.axis_index("occ")
+        chip, core = occ // 2, occ % 2
+        active = (core + plane) % 2 == 1
+        place = jnp.stack([plane, chip, core, active.astype(jnp.int32)]).astype(jnp.int32)
+        both = ("occ", "ao")
+        whole_vmem = pl.BlockSpec(memory_space=pltpu.VMEM)
+        whole_smem = pl.BlockSpec(memory_space=pltpu.SMEM)
+
+        def send(x, pairs):
+            return lax.ppermute(x, both, pairs)
+
+        def call(body, inputs, outputs, scratch=(), flops=0, moved=0, far_inputs=0, out_space=None):
+            near_inputs = len(inputs) - far_inputs
+            return pl.pallas_call(
+                body,
+                out_shape=[jax.ShapeDtypeStruct(s, d) for s, d in outputs],
+                in_specs=[whole_smem] + [whole_vmem] * near_inputs + [hbm] * far_inputs,
+                out_specs=[out_space or whole_vmem] * len(outputs),
+                scratch_shapes=list(scratch),
+                cost_estimate=pl.CostEstimate(flops=flops, bytes_accessed=moved, transcendentals=0),
+                compiler_params=pltpu.CompilerParams(vmem_limit_bytes=VMEM_LIMIT),
+            )(place, *inputs)
+
+        hbm = pl.BlockSpec(memory_space=pl.ANY)
+        in_hbm = pl.BlockSpec(memory_space=pltpu.HBM)
+
+        def group_copies(source, to, sems):
+            rows = [pl.ds(g * group, group) for g in range(groups)]
+            return [pltpu.make_async_copy(source.at[r, :], to.at[r, :], sems.at[g]) for g, r in enumerate(rows)]
+
+        def fit_in_place(metric_ref, ints_ref, copies, turned_ref=None):
+            for g, copy in enumerate(copies):
+                copy.wait()
+                rows = slice(g * group, (g + 1) * group)
+                value = jnp.dot(metric_ref[g], ints_ref[rows, :], preferred_element_type=f32).astype(bf16)
+                ints_ref[rows, :] = value
+                if turned_ref is not None:
+                    turned_ref[:, rows] = value.T
+
+        def put_halves(at, stage_ref, own_hbm, give_hbm, j, sems, act):
+            for h in range(2):
+                part = stage_ref.at[j, :, pl.ds(h * half, half)]
+
+                @pl.when(at[2] == h)
+                def _():
+                    act(pltpu.make_async_copy(part, own_hbm.at[j], sems.at[j, h]))
+
+                @pl.when(at[2] != h)
+                def _():
+                    act(pltpu.make_async_copy(part, give_hbm.at[j], sems.at[j, h]))
+
+        def start(copy):
+            copy.start()
+
+        def wait(copy):
+            copy.wait()
+
+        def product(turned_ref, right_ref):
+            return jnp.dot(turned_ref[...], right_ref[...], preferred_element_type=f32).astype(bf16)
+
+        raw = half_ints[0]
+        low = send(raw, one_core([(0, 0, 1), (0, 2, 3), (1, 1, 2)]))
+        high = send(raw, one_core([(0, 2, 1), (1, 1, 0), (1, 3, 2)]))
+        far = send(raw, one_core([(0, 3, 1), (1, 0, 2)]))
+
+        live = jnp.arange(slots, dtype=jnp.int32) < dom_len[0]
+        metric = jnp.where(live[:, None, None], metric_inv[dom_blocks[0]], 0)
+        wide = 2 if slots % 2 == 0 else 1
+        groups, group = slots // wide, wide * block
+        on_diagonal = jnp.eye(wide, dtype=bool)[None, :, None, :, None]
+        metric_wide = jnp.where(
+            on_diagonal, metric.reshape(groups, wide, block, 1, block), jnp.zeros((), bf16)
+        ).reshape(groups, group, group)
+        mine = (
+            jnp.einsum("sab,sbm->sam", metric, raw.reshape(slots, block, ao_rows), preferred_element_type=f32)
+            .reshape(domain, ao_rows)
+            .astype(bf16)
+        )
+        mine_turned = mine.T
+        pair = jnp.einsum("pm,m->p", mine, coef[:, 0], preferred_element_type=f32)
+        one_hot = dom_blocks[0][:, None] == jnp.arange(fit_blocks, dtype=jnp.int32)
+        density = jnp.einsum(
+            "sf,sr->fr",
+            one_hot.astype(f32),
+            pair.reshape(slots, block),
+            precision=lax.Precision.HIGHEST,
+        )
+        for axis, n, bit in (("occ", n_occ, 1), ("occ", n_occ, 2), ("occ", n_occ, 4), ("ao", n_ao, 1), ("ao", n_ao, 2)):
+            density = density + lax.ppermute(density, axis, [(i, i ^ bit) for i in range(n)])
+
+        square = jnp.einsum("pm,pn->mn", mine, mine, preferred_element_type=f32)
+        keep = lax.dynamic_slice_in_dim(square, core * half, half, 1)
+        give = lax.dynamic_slice_in_dim(square, (1 - core) * half, half, 1).astype(bf16)
+        swap = [(i, i ^ 1) for i in range(n_occ)]
+        got = lax.ppermute(give, "occ", swap)
+        square = (keep + got.astype(f32)).astype(bf16)
+        to_sibling = [(device(c, (p + 1) % 2, p), device(c, p % 2, p)) for p in range(n_ao) for c in range(chips)]
+
+        def near_body(
+            at, metric_ref, turned_ref, low_hbm, high_hbm,
+            own_hbm, give_hbm, outer_hbm,
+            low_ref, high_ref, low_turned, high_turned, stage, in_sems, out_sems, outer_sem,
+        ):
+            plane_now, busy = at[0], at[3] == 1
+            has_low, has_high = busy & (plane_now >= 1), busy & (plane_now <= n_ao - 2)
+            low_copies = group_copies(low_hbm, low_ref, in_sems.at[0])
+            high_copies = group_copies(high_hbm, high_ref, in_sems.at[1])
+
+            @pl.when(has_low)
+            def _():
+                for copy in low_copies:
+                    copy.start()
+
+            @pl.when(has_high)
+            def _():
+                for copy in high_copies:
+                    copy.start()
+
+            @pl.when(has_low)
+            def _():
+                fit_in_place(metric_ref, low_ref, low_copies, low_turned)
+                stage[0] = product(turned_ref, low_ref)
+                put_halves(at, stage, own_hbm, give_hbm, 0, out_sems, start)
+
+            @pl.when(has_high)
+            def _():
+                fit_in_place(metric_ref, high_ref, high_copies, high_turned)
+                stage[1] = product(turned_ref, high_ref)
+                put_halves(at, stage, own_hbm, give_hbm, 1, out_sems, start)
+
+            low_outer = pltpu.make_async_copy(low_turned, outer_hbm, outer_sem)
+            high_outer = pltpu.make_async_copy(high_turned, outer_hbm, outer_sem)
+
+            @pl.when(has_low & has_high)
+            def _():
+                @pl.when(plane_now == 1)
+                def _():
+                    low_outer.start()
+
+                @pl.when(plane_now != 1)
+                def _():
+                    high_outer.start()
+
+                stage[2] = product(low_turned, high_ref)
+                put_halves(at, stage, own_hbm, give_hbm, 2, out_sems, start)
+
+            @pl.when(has_low)
+            def _():
+                put_halves(at, stage, own_hbm, give_hbm, 0, out_sems, wait)
+
+            @pl.when(has_high)
+            def _():
+                put_halves(at, stage, own_hbm, give_hbm, 1, out_sems, wait)
+
+            @pl.when(has_low & has_high)
+            def _():
+                low_outer.wait()
+                put_halves(at, stage, own_hbm, give_hbm, 2, out_sems, wait)
+
+        piece = (ao_rows, half)
+        fitted = (domain, ao_rows)
+        product_flops = 2 * domain * ao_rows * ao_rows
+        square_tile = (ao_rows, ao_rows)
+        own, give, outer = call(
+            near_body,
+            [metric_wide, mine_turned, low, high],
+            [((3, *piece), bf16), ((3, *piece), bf16), (fitted[::-1], bf16)],
+            [
+                pltpu.VMEM(fitted, bf16),
+                pltpu.VMEM(fitted, bf16),
+                pltpu.VMEM(fitted[::-1], bf16),
+                pltpu.VMEM(fitted[::-1], bf16),
+                pltpu.VMEM((3, *square_tile), bf16),
+                pltpu.SemaphoreType.DMA((2, groups)),
+                pltpu.SemaphoreType.DMA((3, 2)),
+                pltpu.SemaphoreType.DMA,
+            ],
+            3 * product_flops,
+            6 * 2**20,
+            far_inputs=2,
+            out_space=in_hbm,
+        )
+        got = send(give, to_sibling)
+
+        def pick(own_all, got_all, alone, index_of):
+            count = own_all.shape[0]
+
+            def body(at, own_hbm, got_hbm, alone_hbm, *rest):
+                outs, sems = rest[:chips], rest[chips]
+                busy = at[3] == 1
+                for k in range(chips):
+                    j = index_of(at[0], at[1] ^ k)
+                    safe = jnp.clip(j, 0, count - 1)
+                    mine_copy = pltpu.make_async_copy(own_hbm.at[safe], outs[k], sems.at[k])
+                    got_copy = pltpu.make_async_copy(got_hbm.at[safe], outs[k], sems.at[k])
+                    alone_copy = pltpu.make_async_copy(alone_hbm, outs[k], sems.at[k])
+
+                    @pl.when((j >= 0) & busy)
+                    def _():
+                        mine_copy.start()
+
+                    @pl.when((j >= 0) & jnp.logical_not(busy))
+                    def _():
+                        got_copy.start()
+
+                    @pl.when(j < 0)
+                    def _():
+                        alone_copy.start()
+
+                for k in range(chips):
+                    pltpu.make_async_copy(alone_hbm, outs[k], sems.at[k]).wait()
+
+            return call(
+                body,
+                [own_all, got_all, alone],
+                [(piece, bf16)] * chips,
+                [pltpu.SemaphoreType.DMA((chips,))],
+                0,
+                2 * 2**20,
+                far_inputs=3,
+            )
+
+        def early_index(plane_now, goal):
+            away = goal - plane_now
+            one = jnp.where(away == -1, 0, jnp.where(away == 1, 1, 2))
+            return jnp.where(away == 0, -1, one)
+
+        picked = pick(own, got, square, early_index)
+        early_in = [picked[0]]
+        for k in range(1, chips):
+            moves = [((p, c ^ k), (p, c)) for p, c in spots if early_owner(p, c)]
+            early_in.append(send(picked[k], both_cores(moves)))
+
+        def sum_body(at, a_ref, b_ref, c_ref, d_ref, total_ref, same_ref, other_ref, full):
+            core_now = at[2]
+            full[...] = (
+                a_ref[...].astype(f32) + b_ref[...].astype(f32) + c_ref[...].astype(f32) + d_ref[...].astype(f32)
+            )
+            total_ref[...] = full[...].astype(bf16)
+            for h in range(2):
+                turned = full[h * half : (h + 1) * half, :].T.astype(bf16)
+
+                @pl.when(core_now == h)
+                def _():
+                    same_ref[...] = turned
+
+                @pl.when(core_now != h)
+                def _():
+                    other_ref[...] = turned
+
+        corner = (half, half)
+
+        def sum_up(parts):
+            return call(
+                sum_body, parts, [(piece, bf16), (corner, bf16), (corner, bf16)], [pltpu.VMEM(piece, f32)], 0, 2 * 2**20
+            )
+
+        early, early_same, early_other = sum_up(early_in)
+
+        def far_body(
+            at, metric_ref, turned_ref, outer_hbm, far_hbm,
+            own_hbm, give_hbm,
+            far_ref, outer_ref, stage, in_sems, out_sems, outer_sem,
+        ):
+            copies = group_copies(far_hbm, far_ref, in_sems)
+            outer_copy = pltpu.make_async_copy(outer_hbm, outer_ref, outer_sem)
+
+            @pl.when((at[3] == 1) & (at[0] >= 1) & (at[0] <= n_ao - 2))
+            def _():
+                for copy in copies:
+                    copy.start()
+                outer_copy.start()
+                fit_in_place(metric_ref, far_ref, copies)
+                stage[0] = product(turned_ref, far_ref)
+                put_halves(at, stage, own_hbm, give_hbm, 0, out_sems, start)
+                outer_copy.wait()
+                stage[1] = product(outer_ref, far_ref)
+                put_halves(at, stage, own_hbm, give_hbm, 1, out_sems, start)
+                put_halves(at, stage, own_hbm, give_hbm, 0, out_sems, wait)
+                put_halves(at, stage, own_hbm, give_hbm, 1, out_sems, wait)
+
+        late_own, late_give = call(
+            far_body,
+            [metric_wide, mine_turned, outer, far],
+            [((2, *piece), bf16), ((2, *piece), bf16)],
+            [
+                pltpu.VMEM(fitted, bf16),
+                pltpu.VMEM(fitted[::-1], bf16),
+                pltpu.VMEM((2, *square_tile), bf16),
+                pltpu.SemaphoreType.DMA((groups,)),
+                pltpu.SemaphoreType.DMA((2, 2)),
+                pltpu.SemaphoreType.DMA,
+            ],
+            2 * product_flops,
+            4 * 2**20,
+            far_inputs=2,
+            out_space=in_hbm,
+        )
+        late_pairs = [(device(c, (p + 1) % 2, p), device(c, p % 2, p)) for p in middle for c in range(chips)]
+        late_got = send(late_give, late_pairs)
+
+        def late_index(plane_now, goal):
+            return jnp.where(goal == plane_now ^ 2, 0, 1)
+
+        picked = pick(late_own, late_got, square, late_index)
+        late_in = [picked[0]]
+        for k in range(1, chips):
+            moves = [((p, p ^ 2 ^ k), (p, p ^ 2)) for p in middle]
+            moves += [((p, p ^ 3 ^ k), (p, p ^ 3)) for p in middle]
+            late_in.append(send(picked[k], both_cores(moves)))
+        late, late_same, late_other = sum_up(late_in)
+
+        arrived = [
+            send(early_same, both_cores(early_turn)),
+            send(early_other, both_cores(early_turn, 1)),
+            send(early, both_cores(early_straight)),
+            send(late_same, both_cores(late_turn)),
+            send(late_other, both_cores(late_turn, 1)),
+            send(late, both_cores(late_straight)),
+        ]
+
+        def last_body(at, early_ref, late_ref, es, eo, ed, ls, lo, ld, out_ref):
+            plane_now, chip_now, core_now = at[0], at[1], at[2]
+            gap = jnp.abs(plane_now - chip_now)
+            in_middle = (plane_now >= 1) & (plane_now <= n_ao - 2)
+            out_ref[...] = ed[...].astype(f32) + ld[...].astype(f32)
+
+            @pl.when(gap <= 1)
+            def _():
+                out_ref[...] += early_ref[...].astype(f32)
+
+            @pl.when((gap == 2) & in_middle)
+            def _():
+                out_ref[...] += late_ref[...].astype(f32)
+
+            same_rows = pl.ds(pl.multiple_of(core_now * half, half), half)
+            other_rows = pl.ds(pl.multiple_of((1 - core_now) * half, half), half)
+            out_ref[same_rows, :] += es[...].astype(f32) + ls[...].astype(f32)
+            out_ref[other_rows, :] += eo[...].astype(f32) + lo[...].astype(f32)
+
+        (exchange_k,) = call(last_body, [early, late, *arrived], [(piece, f32)], [], 0, 3 * 2**20)
+        return exchange_k, density.reshape(fit_blocks * block)
+
+    return on_device
+
+
 def solution(mesh):
+    n_occ, n_ao = mesh.shape["occ"], mesh.shape["ao"]
     in_specs = (P("ao", "occ"), P("occ", None, "ao"), P(), P("occ", None), P("occ"))
     out_specs = (P("ao", "occ"), P())
-    return jax.shard_map(
-        on_device, mesh=mesh, in_specs=in_specs, out_specs=out_specs, check_vma=False
-    )
+
+    def sharded(body):
+        return jax.shard_map(body, mesh=mesh, in_specs=in_specs, out_specs=out_specs, check_vma=False)
+
+    if not (n_ao == 4 and n_occ == 2 * n_ao):
+        return sharded(general_plan)
+
+    def whole(*args):
+        if args[1].shape[0] != n_occ:
+            return sharded(general_plan)(*args)
+        return sharded(line_plan(n_occ, n_ao))(*args)
+
+    return whole

time: 160 us -> 114 us (0.71)
  the two profiles are of different devices: /device:TPU:0 before, /device:TPU:13 now
where the time goes in v1:
time: 114 us
  starting transfers between devices  69.6 us (61%)
  waiting for transfers between devices  17.5 us (15%)
  local copies, waits for them, and re-layouts  7.12 us (6%)
  Pallas kernels  7.01 us (6%)
  matrix products  6.92 us (6%)
  other arithmetic  3.77 us (3%)
  between operations  1.78 us (2%)
    ppermute x17, starting transfers between devices, send(): return lax.ppermute(x, both, pairs)  45.1 us
    ppermute x1, starting transfers between devices, on_device(): got = lax.ppermute(give, 'occ', swap)  19.3 us
    ppermute x17, waiting for transfers between devices, send(): return lax.ppermute(x, both, pairs)  10.9 us
    pallas_call x7, Pallas kernels, call(): pl.pallas_call(body, out_shape=[jax.ShapeDtypeStruct(s, d) for s, d in ou...  7.01 us
    ppermute x5, waiting for transfers between devices, on_device(): lax.ppermute(density, axis, [(i, i ^ bit) for i in range(n)])  6.42 us
    ppermute x5, starting transfers between devices, on_device(): lax.ppermute(density, axis, [(i, i ^ bit) for i in range(n)])  5.16 us
    unnamed x17, local copies, waits for them, and re-layouts  2.76 us
    dot_general x1, matrix products, on_device(): jnp.einsum('sab,sbm->sam', metric, raw.reshape(slots, block, ao_rows), pr...  2.68 us
  transfers between devices with their start and end apart: 23, of which 6 were waited for; matrix products, arithmetic and copies ran while one was open for 13% of the time, Pallas kernels for 4%

profile of v1, /device:TPU:13, one launch (start us, length us, event | category | flops | bytes accessed | tf_op | source)
XLA Modules:
  0.0 113.6 jit_solution(100230423336972577)
XLA Ops:
  0.6 4.3 %collective-permute-start = (bf16[1024,512]{1,0:T(8,128)(2,1)}, bf16[1024,512]{1,0:T(8,128)(2,1)}, u32[]{:S(2)}, u32[]{:S(2)}) collective-permute-start(bf16[1024,512]{1,0:T(8,128)(2,1)} %bitcast.40), channel_id=1, source_target_pairs={{0,1},{8,9},{16,17},{24,25},{2,3},{10,11},{18,19},{26,27},{5,6},{1... | collective-permute-start | bytes 3145736 | tf_op jit(solution)/shard_map/ppermute | solution.py:89
  5.0 2.3 %collective-permute-start.1 = (bf16[1024,512]{1,0:T(8,128)(2,1)}, bf16[1024,512]{1,0:T(8,128)(2,1)}, u32[]{:S(2)}, u32[]{:S(2)}) collective-permute-start(bf16[1024,512]{1,0:T(8,128)(2,1)} %bitcast.41), channel_id=1, source_target_pairs={{2,1},{10,9},{18,17},{26,25},{5,4},{13,12},{21,20},{29,28},{7,6},{... | collective-permute-start | bytes 3145736 | tf_op jit(solution)/shard_map/ppermute | solution.py:89
  7.2 1.6 %collective-permute-start.7 = (bf16[1024,512]{1,0:T(8,128)(2,1)}, bf16[1024,512]{1,0:T(8,128)(2,1)}, u32[]{:S(2)}, u32[]{:S(2)}) collective-permute-start(bf16[1024,512]{1,0:T(8,128)(2,1)} %bitcast.42), channel_id=1, source_target_pairs={{3,1},{11,9},{19,17},{27,25},{4,6},{12,14},{20,22},{28,30}} | collective-permute-start | bytes 3145736 | tf_op jit(solution)/shard_map/ppermute | solution.py:89
  8.8 0.7 fusion.7
  10.2 0.6 gather_fusion
  11.2 1.1 broadcast_in_dim.52
  12.5 2.7 %convolution_convert_fusion = bf16[8,128,512]{2,1,0:T(8,128)(2,1)} fusion(bf16[8,128,512]{2,1,0:T(8,128)(2,1)} %bitcast.43, bf16[8,128,128]{2,1,0:T(8,128)(2,1)S(1)} %gather_fusion, pred[8]{0:T(512)(128)(4,1)S(1)} %iota_compare_fusion.3), kind=kOutput, calls=%fused_computation.1 | convolution fusion | flops 134873088 | bytes 2359304 | tf_op jit(solution)/shard_map/sab,sbm->sam/dot_general | solution.py:154
  15.2 1.5 %copy.13 = bf16[1024,512]{0,1:T(8,128)(2,1)S(1)} copy(bf16[1024,512]{1,0:T(8,128)(2,1)} %bitcast.38) | data formatting | bytes 2097152 | tf_op jit(solution)/shard_map/convert_element_type | solution.py:156
  16.8 1.1 broadcast_select_fusion.metric_ref
  17.9 2.4 %convolution_bitcast_fusion = f32[512,512]{1,0:T(8,128)S(1)} fusion(bf16[8,128,512]{2,1,0:T(8,128)(2,1)} %convolution_convert_fusion), kind=kOutput, calls=%fused_computation.2 | convolution fusion | flops 536870912 | bytes 2097152 | tf_op jit(solution)/shard_map/pm,pn->mn/dot_general | solution.py:170
  20.3 3.3 %collective-permute-done.low_hbm = bf16[1024,512]{1,0:T(8,128)(2,1)} collective-permute-done((bf16[1024,512]{1,0:T(8,128)(2,1)}, bf16[1024,512]{1,0:T(8,128)(2,1)}, u32[]{:S(2)}, u32[]{:S(2)}) %collective-permute-start) | collective-permute-done | bytes 1048608 | tf_op jit(solution)/shard_map/ppermute | solution.py:89
  23.6 0.8 shard_map.68
  24.4 0.9 copy-done.1
  25.3 0.6 shard_map.71
  25.9 0.8 copy-done.3
  26.7 1.4 %collective-permute-start.8 = (bf16[2,512,256]{2,1,0:T(8,128)(2,1)}, bf16[2,512,256]{2,1,0:T(8,128)(2,1)S(1)}, u32[]{:S(2)}, u32[]{:S(2)}) collective-permute-start(bf16[2,512,256]{2,1,0:T(8,128)(2,1)} %get-tuple-element.30), channel_id=1, source_target_pairs={{1,5},{9,13},{17,21},{25,29},{6,2},{14,10},{22,18},{30,26}} | collective-permute-start | bytes 1572872 | tf_op jit(solution)/shard_map/ppermute | solution.py:89
  28.1 0.7 dynamic-slice_convert_fusion
  28.9 19.3 %collective-permute-start.3 = (bf16[512,256]{1,0:T(8,128)(2,1)}, bf16[512,256]{1,0:T(8,128)(2,1)}, u32[]{:S(2)}, u32[]{:S(2)}) collective-permute-start(bf16[512,256]{1,0:T(8,128)(2,1)} %dynamic-slice_convert_fusion), channel_id=1, source_target_pairs={{0,4},{4,0},{8,12},{12,8},{16,20},{20,16},{24,28},{28,24},{1,5},{5... | collective-permute-start | bytes 786440 | tf_op jit(solution)/shard_map/ppermute | solution.py:174
  48.1 1.3 %collective-permute-start.2 = (bf16[3,512,256]{2,1,0:T(8,128)(2,1)}, bf16[3,512,256]{2,1,0:T(8,128)(2,1)}, u32[]{:S(2)}, u32[]{:S(2)}) collective-permute-start(bf16[3,512,256]{2,1,0:T(8,128)(2,1)} %get-tuple-element.22), channel_id=1, source_target_pairs={{4,0},{12,8},{20,16},{28,24},{1,5},{9,13},{17,21},{25,29},{6,2},{1... | collective-permute-start | bytes 2359304 | tf_op jit(solution)/shard_map/ppermute | solution.py:89
  49.7 1.2 %add_convert_fusion.alone_hbm = bf16[512,256]{1,0:T(8,128)(2,1)S(1)} fusion(bf16[512,256]{1,0:T(8,128)(2,1)} %collective-permute-done.3, f32[512,512]{1,0:T(8,128)} %copy-done.5, s32[]{:T(128)S(6)} %select_n.53), kind=kLoop, calls=%fused_computation.3 | loop fusion | flops 393216 | bytes 1048580 | tf_op jit(solution)/shard_map/convert_element_type | solution.py:175
  50.9 1.0 copy-done.4
  51.9 0.7 shard_map.72
  52.6 3.1 %collective-permute-start.9 = (bf16[512,256]{1,0:T(8,128)(2,1)S(1)}, bf16[512,256]{1,0:T(8,128)(2,1)S(1)}, u32[]{:S(2)}, u32[]{:S(2)}) collective-permute-start(bf16[512,256]{1,0:T(8,128)(2,1)S(1)} %get-tuple-element.32), channel_id=1, source_target_pairs={{17,25},{21,29},{10,2},{14,6},{25,17},{29,21},{2,10},{6,14}} | collective-permute-start | bytes 786440 | tf_op jit(solution)/shard_map/ppermute | solution.py:89
  55.7 1.6 %fusion.4 = f32[1,8,128]{2,0,1:T(1,128)S(1)} fusion(bf16[8,128,512]{2,1,0:T(8,128)(2,1)} %convolution_convert_fusion, bf16[512,1]{0,1:T(2,128)(2,1)S(1)} %copy-done.6), kind=kOutput, calls=%fused_computation.16 | convolution fusion | flops 1048576 | bytes 1053696 | tf_op jit(solution)/shard_map/pm,m->p/dot_general | solution.py:159
  57.3 1.3 %collective-permute-start.10 = (bf16[512,256]{1,0:T(8,128)(2,1)S(1)}, bf16[512,256]{1,0:T(8,128)(2,1)S(1)}, u32[]{:S(2)}, u32[]{:S(2)}) collective-permute-start(bf16[512,256]{1,0:T(8,128)(2,1)S(1)} %get-tuple-element.33), channel_id=1, source_target_pairs={{9,25},{13,29},{18,2},{22,6},{1,17},{5,21},{26,10},{30,14}} | collective-permute-start | bytes 786440 | tf_op jit(solution)/shard_map/ppermute | solution.py:89
  58.6 1.3 %collective-permute-start.11 = (bf16[512,256]{1,0:T(8,128)(2,1)S(1)}, bf16[512,256]{1,0:T(8,128)(2,1)S(1)}, u32[]{:S(2)}, u32[]{:S(2)}) collective-permute-start(bf16[512,256]{1,0:T(8,128)(2,1)S(1)} %get-tuple-element.34), channel_id=1, source_target_pairs={{1,25},{5,29},{26,2},{30,6},{9,17},{13,21},{18,10},{22,14}} | collective-permute-start | bytes 786440 | tf_op jit(solution)/shard_map/ppermute | solution.py:89
  60.0 0.3 fusion.3
  60.2 2.2 %collective-permute-start.18 = (f32[64,128]{1,0:T(8,128)S(1)}, f32[64,128]{1,0:T(8,128)S(1)}, u32[]{:S(2)}, u32[]{:S(2)}) collective-permute-start(f32[64,128]{1,0:T(8,128)S(1)} %fusion.3), channel_id=1, source_target_pairs={{0,4},{4,0},{8,12},{12,8},{16,20},{20,16},{24,28},{28,24},{1,5},{5... | collective-permute-start | bytes 98312 | tf_op jit(solution)/shard_map/ppermute | solution.py:168
  62.4 1.7 %shard_map.69 = (bf16[512,256]{1,0:T(8,128)(2,1)S(1)}, bf16[512,256]{1,0:T(8,128)(2,1)S(1)}, bf16[512,256]{1,0:T(8,128)(2,1)S(1)}, bf16[512,256]{1,0:T(8,128)(2,1)S(1)}) custom-call(s32[4]{0:T(128)S(1)} %pad_add_fusion.at, bf16[3,512,256]{2,1,0:T(8,128)(2,1)S(1)} %copy-done.2, bf16[3,512,256]{2,1,0:T(8,128)(2,1)} %collective-permute-done.2.got_hbm, ...), custom_call_target="tpu_custom_call" | custom-call | bytes 2097152 | tf_op jit(solution)/shard_map/pallas_call | solution.py:93
  64.1 2.2 %collective-permute-start.4 = (bf16[512,256]{1,0:T(8,128)(2,1)S(1)}, bf16[512,256]{1,0:T(8,128)(2,1)S(1)}, u32[]{:S(2)}, u32[]{:S(2)}) collective-permute-start(bf16[512,256]{1,0:T(8,128)(2,1)S(1)} %get-tuple-element.24), channel_id=1, source_target_pairs={{8,0},{12,4},{0,8},{4,12},{9,1},{13,5},{1,9},{5,13},{25,17},{29,21... | collective-permute-start | bytes 786440 | tf_op jit(solution)/shard_map/ppermute | solution.py:89
  66.3 5.3 %collective-permute-start.5 = (bf16[512,256]{1,0:T(8,128)(2,1)S(1)}, bf16[512,256]{1,0:T(8,128)(2,1)S(1)}, u32[]{:S(2)}, u32[]{:S(2)}) collective-permute-start(bf16[512,256]{1,0:T(8,128)(2,1)S(1)} %get-tuple-element.25), channel_id=1, source_target_pairs={{16,0},{20,4},{24,8},{28,12},{17,1},{21,5},{25,9},{29,13},{1,17},{... | collective-permute-start | bytes 786440 | tf_op jit(solution)/shard_map/ppermute | solution.py:89
  71.6 1.9 %collective-permute-start.6 = (bf16[512,256]{1,0:T(8,128)(2,1)S(1)}, bf16[512,256]{1,0:T(8,128)(2,1)S(1)}, u32[]{:S(2)}, u32[]{:S(2)}) collective-permute-start(bf16[512,256]{1,0:T(8,128)(2,1)S(1)} %get-tuple-element.26), channel_id=1, source_target_pairs={{24,0},{28,4},{16,8},{20,12},{25,1},{29,5},{17,9},{21,13},{9,17},{... | collective-permute-start | bytes 786440 | tf_op jit(solution)/shard_map/ppermute | solution.py:89
  73.5 1.2 %collective-permute-start.19 = (f32[64,128]{1,0:T(8,128)S(1)}, f32[64,128]{1,0:T(8,128)S(1)}, u32[]{:S(2)}, u32[]{:S(2)}) collective-permute-start(f32[64,128]{1,0:T(8,128)S(1)} %add.53), channel_id=1, source_target_pairs={{0,8},{4,12},{8,0},{12,4},{16,24},{20,28},{24,16},{28,20},{1,9},{5... | collective-permute-start | bytes 98312 | tf_op jit(solution)/shard_map/ppermute | solution.py:168
  74.8 0.8 shard_map.73
  75.6 1.3 %collective-permute-start.15 = (bf16[256,256]{1,0:T(8,128)(2,1)S(1)}, bf16[256,256]{1,0:T(8,128)(2,1)S(1)}, u32[]{:S(2)}, u32[]{:S(2)}) collective-permute-start(bf16[256,256]{1,0:T(8,128)(2,1)S(1)} %get-tuple-element.38), channel_id=1, source_target_pairs={{25,11},{29,15},{2,16},{6,20},{17,3},{21,7},{10,24},{14,28}} | collective-permute-start | bytes 393224 | tf_op jit(solution)/shard_map/ppermute | solution.py:89
  76.9 5.1 %collective-permute-done.19 = f32[64,128]{1,0:T(8,128)S(1)} collective-permute-done((f32[64,128]{1,0:T(8,128)S(1)}, f32[64,128]{1,0:T(8,128)S(1)}, u32[]{:S(2)}, u32[]{:S(2)}) %collective-permute-start.19) | collective-permute-done | bytes 32800 | tf_op jit(solution)/shard_map/ppermute | solution.py:168
  82.0 1.7 %collective-permute-start.20 = (f32[64,128]{1,0:T(8,128)S(1)}, f32[64,128]{1,0:T(8,128)S(1)}, u32[]{:S(2)}, u32[]{:S(2)}) collective-permute-start(f32[64,128]{1,0:T(8,128)S(1)} %add.54), channel_id=1, source_target_pairs={{0,16},{4,20},{8,24},{12,28},{16,0},{20,4},{24,8},{28,12},{1,17},{... | collective-permute-start | bytes 98312 | tf_op jit(solution)/shard_map/ppermute | solution.py:168
  83.7 1.3 %collective-permute-done.20 = f32[64,128]{1,0:T(8,128)S(1)} collective-permute-done((f32[64,128]{1,0:T(8,128)S(1)}, f32[64,128]{1,0:T(8,128)S(1)}, u32[]{:S(2)}, u32[]{:S(2)}) %collective-permute-start.20) | collective-permute-done | bytes 32800 | tf_op jit(solution)/shard_map/ppermute | solution.py:168
  85.0 3.3 %collective-permute-start.17 = (bf16[512,256]{1,0:T(8,128)(2,1)S(1)}, bf16[512,256]{1,0:T(8,128)(2,1)S(1)}, u32[]{:S(2)}, u32[]{:S(2)}) collective-permute-start(bf16[512,256]{1,0:T(8,128)(2,1)S(1)} %get-tuple-element.35.late_ref), channel_id=1, source_target_pairs={{17,24},{21,28},{10,3},{14,7}} | collective-permute-start | bytes 786440 | tf_op jit(solution)/shard_map/ppermute | solution.py:89
  88.4 0.8 shard_map.70
  89.2 0.7 collective-permute-start.14
  90.0 6.1 %collective-permute-start.16 = (bf16[256,256]{1,0:T(8,128)(2,1)S(1)}, bf16[256,256]{1,0:T(8,128)(2,1)S(1)}, u32[]{:S(2)}, u32[]{:S(2)}) collective-permute-start(bf16[256,256]{1,0:T(8,128)(2,1)S(1)} %get-tuple-element.39), channel_id=1, source_target_pairs={{25,15},{29,11},{2,20},{6,16},{17,7},{21,3},{10,28},{14,24}} | collective-permute-start | bytes 393224 | tf_op jit(solution)/shard_map/ppermute | solution.py:89
  96.1 1.9 %collective-permute-start.12 = (bf16[256,256]{1,0:T(8,128)(2,1)S(1)}, bf16[256,256]{1,0:T(8,128)(2,1)S(1)}, u32[]{:S(2)}, u32[]{:S(2)}) collective-permute-start(bf16[256,256]{1,0:T(8,128)(2,1)S(1)} %get-tuple-element.36), channel_id=1, source_target_pairs={{8,1},{12,5},{1,8},{5,12},{17,10},{21,14},{10,17},{14,21},{26,19},... | collective-permute-start | bytes 393224 | tf_op jit(solution)/shard_map/ppermute | solution.py:89
  98.1 5.9 %collective-permute-start.13 = (bf16[256,256]{1,0:T(8,128)(2,1)S(1)}, bf16[256,256]{1,0:T(8,128)(2,1)S(1)}, u32[]{:S(2)}, u32[]{:S(2)}) collective-permute-start(bf16[256,256]{1,0:T(8,128)(2,1)S(1)} %get-tuple-element.37), channel_id=1, source_target_pairs={{8,5},{12,1},{1,12},{5,8},{17,14},{21,10},{10,21},{14,17},{26,23},... | collective-permute-start | bytes 393224 | tf_op jit(solution)/shard_map/ppermute | solution.py:89
  103.9 0.6 add_bitcast_fusion
  104.6 1.3 %collective-permute-done.12.es = bf16[256,256]{1,0:T(8,128)(2,1)S(1)} collective-permute-done((bf16[256,256]{1,0:T(8,128)(2,1)S(1)}, bf16[256,256]{1,0:T(8,128)(2,1)S(1)}, u32[]{:S(2)}, u32[]{:S(2)}) %collective-permute-start.12) | collective-permute-done | bytes 131104 | tf_op jit(solution)/shard_map/ppermute | solution.py:89
  105.8 6.2 %collective-permute-done.13.eo = bf16[256,256]{1,0:T(8,128)(2,1)S(1)} collective-permute-done((bf16[256,256]{1,0:T(8,128)(2,1)S(1)}, bf16[256,256]{1,0:T(8,128)(2,1)S(1)}, u32[]{:S(2)}, u32[]{:S(2)}) %collective-permute-start.13) | collective-permute-done | bytes 131104 | tf_op jit(solution)/shard_map/ppermute | solution.py:89
  112.1 1.6 %shard_map.74 = f32[512,256]{1,0:T(8,128)} custom-call(s32[4]{0:T(128)S(1)} %pad_add_fusion.at, bf16[512,256]{1,0:T(8,128)(2,1)S(1)} %get-tuple-element.27.early_ref, bf16[512,256]{1,0:T(8,128)(2,1)S(1)} %get-tuple-element.35.late_ref, bf16[256,256]{1,0:T(8,128)(2,1)S(1)} %collective-permute-done.12.es, bf16[256,256]{1,0:T(8,128)(2,1)S(1)} %collective-permute-done.13.eo, ...), custom_call_target="tpu_custom_call" | custom-call | bytes 3145728 | tf_op jit(solution)/shard_map/pallas_call | solution.py:93
  (46 shorter events, 1.0 us)
Async XLA Ops:
  0.6 9.6 %copy-start = (bf16[64,128,128]{2,1,0:T(8,128)(2,1)S(1)}, bf16[64,128,128]{2,1,0:T(8,128)(2,1)}, u32[]{:S(2)}) copy-start(bf16[64,128,128]{2,1,0:T(8,128)(2,1)} %param.7) | copy-start | bytes 6291460
  0.6 23.0 %collective-permute-start = (bf16[1024,512]{1,0:T(8,128)(2,1)}, bf16[1024,512]{1,0:T(8,128)(2,1)}, u32[]{:S(2)}, u32[]{:S(2)}) collective-permute-start(bf16[1024,512]{1,0:T(8,128)(2,1)} %bitcast.40), channel_id=1, source_target_pairs={{0,1},{8,9},{16,17},{24,25},{2,3},{10,11},{18,19},{26,27},{5,6},{1... | collective-permute-start | bytes 3145736 | tf_op jit(solution)/shard_map/ppermute | solution.py:89
  5.0 18.6 %collective-permute-start.1 = (bf16[1024,512]{1,0:T(8,128)(2,1)}, bf16[1024,512]{1,0:T(8,128)(2,1)}, u32[]{:S(2)}, u32[]{:S(2)}) collective-permute-start(bf16[1024,512]{1,0:T(8,128)(2,1)} %bitcast.41), channel_id=1, source_target_pairs={{2,1},{10,9},{18,17},{26,25},{5,4},{13,12},{21,20},{29,28},{7,6},{... | collective-permute-start | bytes 3145736 | tf_op jit(solution)/shard_map/ppermute | solution.py:89
  7.2 18.0 %collective-permute-start.7 = (bf16[1024,512]{1,0:T(8,128)(2,1)}, bf16[1024,512]{1,0:T(8,128)(2,1)}, u32[]{:S(2)}, u32[]{:S(2)}) collective-permute-start(bf16[1024,512]{1,0:T(8,128)(2,1)} %bitcast.42), channel_id=1, source_target_pairs={{3,1},{11,9},{19,17},{27,25},{4,6},{12,14},{20,22},{28,30}} | collective-permute-start | bytes 3145736 | tf_op jit(solution)/shard_map/ppermute | solution.py:89
  20.3 7.9 %copy-start.5 = (f32[512,512]{1,0:T(8,128)}, f32[512,512]{1,0:T(8,128)S(1)}, u32[]{:S(2)}) copy-start(f32[512,512]{1,0:T(8,128)S(1)} %convolution_bitcast_fusion) | copy-start | bytes 3145732
  24.4 0.9 copy-start.1
  25.9 0.8 copy-start.3
  26.7 29.0 %copy-start.6 = (bf16[512,1]{0,1:T(2,128)(2,1)S(1)}, bf16[512,1]{0,1:T(2,128)(2,1)}, u32[]{:S(2)}) copy-start(bf16[512,1]{0,1:T(2,128)(2,1)} %param.5) | copy-start | bytes 3076
  26.7 33.2 %copy-start.7 = (s32[1,8]{1,0:T(1,128)S(1)}, s32[1,8]{1,0:T(1,128)}, u32[]{:S(2)}) copy-start(s32[1,8]{1,0:T(1,128)} %param.8) | copy-start | bytes 100
  26.7 35.7 %copy-start.2 = (bf16[3,512,256]{2,1,0:T(8,128)(2,1)S(1)}, bf16[3,512,256]{2,1,0:T(8,128)(2,1)}, u32[]{:S(2)}) copy-start(bf16[3,512,256]{2,1,0:T(8,128)(2,1)} %copy-done.1) | copy-start | bytes 2359300
  26.7 24.1 %collective-permute-start.8 = (bf16[2,512,256]{2,1,0:T(8,128)(2,1)}, bf16[2,512,256]{2,1,0:T(8,128)(2,1)S(1)}, u32[]{:S(2)}, u32[]{:S(2)}) collective-permute-start(bf16[2,512,256]{2,1,0:T(8,128)(2,1)} %get-tuple-element.30), channel_id=1, source_target_pairs={{1,5},{9,13},{17,21},{25,29},{6,2},{14,10},{22,18},{30,26}} | collective-permute-start | bytes 1572872 | tf_op jit(solution)/shard_map/ppermute | solution.py:89
  28.9 20.8 %collective-permute-start.3 = (bf16[512,256]{1,0:T(8,128)(2,1)}, bf16[512,256]{1,0:T(8,128)(2,1)}, u32[]{:S(2)}, u32[]{:S(2)}) collective-permute-start(bf16[512,256]{1,0:T(8,128)(2,1)} %dynamic-slice_convert_fusion), channel_id=1, source_target_pairs={{0,4},{4,0},{8,12},{12,8},{16,20},{20,16},{24,28},{28,24},{1,5},{5... | collective-permute-start | bytes 786440 | tf_op jit(solution)/shard_map/ppermute | solution.py:174
  48.1 14.3 %collective-permute-start.2 = (bf16[3,512,256]{2,1,0:T(8,128)(2,1)}, bf16[3,512,256]{2,1,0:T(8,128)(2,1)}, u32[]{:S(2)}, u32[]{:S(2)}) collective-permute-start(bf16[3,512,256]{2,1,0:T(8,128)(2,1)} %get-tuple-element.22), channel_id=1, source_target_pairs={{4,0},{12,8},{20,16},{28,24},{1,5},{9,13},{17,21},{25,29},{6,2},{1... | collective-permute-start | bytes 2359304 | tf_op jit(solution)/shard_map/ppermute | solution.py:89
  50.8 1.0 copy-start.4
  52.6 19.0 %collective-permute-start.9 = (bf16[512,256]{1,0:T(8,128)(2,1)S(1)}, bf16[512,256]{1,0:T(8,128)(2,1)S(1)}, u32[]{:S(2)}, u32[]{:S(2)}) collective-permute-start(bf16[512,256]{1,0:T(8,128)(2,1)S(1)} %get-tuple-element.32), channel_id=1, source_target_pairs={{17,25},{21,29},{10,2},{14,6},{25,17},{29,21},{2,10},{6,14}} | collective-permute-start | bytes 786440 | tf_op jit(solution)/shard_map/ppermute | solution.py:89
  57.3 16.2 %collective-permute-start.10 = (bf16[512,256]{1,0:T(8,128)(2,1)S(1)}, bf16[512,256]{1,0:T(8,128)(2,1)S(1)}, u32[]{:S(2)}, u32[]{:S(2)}) collective-permute-start(bf16[512,256]{1,0:T(8,128)(2,1)S(1)} %get-tuple-element.33), channel_id=1, source_target_pairs={{9,25},{13,29},{18,2},{22,6},{1,17},{5,21},{26,10},{30,14}} | collective-permute-start | bytes 786440 | tf_op jit(solution)/shard_map/ppermute | solution.py:89
  58.6 16.1 %collective-permute-start.11 = (bf16[512,256]{1,0:T(8,128)(2,1)S(1)}, bf16[512,256]{1,0:T(8,128)(2,1)S(1)}, u32[]{:S(2)}, u32[]{:S(2)}) collective-permute-start(bf16[512,256]{1,0:T(8,128)(2,1)S(1)} %get-tuple-element.34), channel_id=1, source_target_pairs={{1,25},{5,29},{26,2},{30,6},{9,17},{13,21},{18,10},{22,14}} | collective-permute-start | bytes 786440 | tf_op jit(solution)/shard_map/ppermute | solution.py:89
  60.2 6.1 %collective-permute-start.18 = (f32[64,128]{1,0:T(8,128)S(1)}, f32[64,128]{1,0:T(8,128)S(1)}, u32[]{:S(2)}, u32[]{:S(2)}) collective-permute-start(f32[64,128]{1,0:T(8,128)S(1)} %fusion.3), channel_id=1, source_target_pairs={{0,4},{4,0},{8,12},{12,8},{16,20},{20,16},{24,28},{28,24},{1,5},{5... | collective-permute-start | bytes 98312 | tf_op jit(solution)/shard_map/ppermute | solution.py:168
  64.1 20.9 %collective-permute-start.4 = (bf16[512,256]{1,0:T(8,128)(2,1)S(1)}, bf16[512,256]{1,0:T(8,128)(2,1)S(1)}, u32[]{:S(2)}, u32[]{:S(2)}) collective-permute-start(bf16[512,256]{1,0:T(8,128)(2,1)S(1)} %get-tuple-element.24), channel_id=1, source_target_pairs={{8,0},{12,4},{0,8},{4,12},{9,1},{13,5},{1,9},{5,13},{25,17},{29,21... | collective-permute-start | bytes 786440 | tf_op jit(solution)/shard_map/ppermute | solution.py:89
  66.3 22.1 %collective-permute-start.5 = (bf16[512,256]{1,0:T(8,128)(2,1)S(1)}, bf16[512,256]{1,0:T(8,128)(2,1)S(1)}, u32[]{:S(2)}, u32[]{:S(2)}) collective-permute-start(bf16[512,256]{1,0:T(8,128)(2,1)S(1)} %get-tuple-element.25), channel_id=1, source_target_pairs={{16,0},{20,4},{24,8},{28,12},{17,1},{21,5},{25,9},{29,13},{1,17},{... | collective-permute-start | bytes 786440 | tf_op jit(solution)/shard_map/ppermute | solution.py:89
  71.6 16.8 %collective-permute-start.6 = (bf16[512,256]{1,0:T(8,128)(2,1)S(1)}, bf16[512,256]{1,0:T(8,128)(2,1)S(1)}, u32[]{:S(2)}, u32[]{:S(2)}) collective-permute-start(bf16[512,256]{1,0:T(8,128)(2,1)S(1)} %get-tuple-element.26), channel_id=1, source_target_pairs={{24,0},{28,4},{16,8},{20,12},{25,1},{29,5},{17,9},{21,13},{9,17},{... | collective-permute-start | bytes 786440 | tf_op jit(solution)/shard_map/ppermute | solution.py:89
  73.5 8.5 %collective-permute-start.19 = (f32[64,128]{1,0:T(8,128)S(1)}, f32[64,128]{1,0:T(8,128)S(1)}, u32[]{:S(2)}, u32[]{:S(2)}) collective-permute-start(f32[64,128]{1,0:T(8,128)S(1)} %add.53), channel_id=1, source_target_pairs={{0,8},{4,12},{8,0},{12,4},{16,24},{20,28},{24,16},{28,20},{1,9},{5... | collective-permute-start | bytes 98312 | tf_op jit(solution)/shard_map/ppermute | solution.py:168
  75.6 22.5 %collective-permute-start.15 = (bf16[256,256]{1,0:T(8,128)(2,1)S(1)}, bf16[256,256]{1,0:T(8,128)(2,1)S(1)}, u32[]{:S(2)}, u32[]{:S(2)}) collective-permute-start(bf16[256,256]{1,0:T(8,128)(2,1)S(1)} %get-tuple-element.38), channel_id=1, source_target_pairs={{25,11},{29,15},{2,16},{6,20},{17,3},{21,7},{10,24},{14,28}} | collective-permute-start | bytes 393224 | tf_op jit(solution)/shard_map/ppermute | solution.py:89
  82.0 3.0 %collective-permute-start.20 = (f32[64,128]{1,0:T(8,128)S(1)}, f32[64,128]{1,0:T(8,128)S(1)}, u32[]{:S(2)}, u32[]{:S(2)}) collective-permute-start(f32[64,128]{1,0:T(8,128)S(1)} %add.54), channel_id=1, source_target_pairs={{0,16},{4,20},{8,24},{12,28},{16,0},{20,4},{24,8},{28,12},{1,17},{... | collective-permute-start | bytes 98312 | tf_op jit(solution)/shard_map/ppermute | solution.py:168
  85.0 4.9 %collective-permute-start.21 = (f32[64,128]{1,0:T(8,128)S(1)}, f32[64,128]{1,0:T(8,128)S(1)}, u32[]{:S(2)}, u32[]{:S(2)}) collective-permute-start(f32[64,128]{1,0:T(8,128)S(1)} %add.55), channel_id=1, source_target_pairs={{0,1},{1,0},{2,3},{3,2},{4,5},{5,4},{6,7},{7,6},{8,9},{9,8},{10,11... | collective-permute-start | bytes 98312 | tf_op jit(solution)/shard_map/ppermute | solution.py:168
  85.0 19.5 %collective-permute-start.17 = (bf16[512,256]{1,0:T(8,128)(2,1)S(1)}, bf16[512,256]{1,0:T(8,128)(2,1)S(1)}, u32[]{:S(2)}, u32[]{:S(2)}) collective-permute-start(bf16[512,256]{1,0:T(8,128)(2,1)S(1)} %get-tuple-element.35.late_ref), channel_id=1, source_target_pairs={{17,24},{21,28},{10,3},{14,7}} | collective-permute-start | bytes 786440 | tf_op jit(solution)/shard_map/ppermute | solution.py:89
  89.2 22.9 %collective-permute-start.14 = (bf16[512,256]{1,0:T(8,128)(2,1)S(1)}, bf16[512,256]{1,0:T(8,128)(2,1)S(1)}, u32[]{:S(2)}, u32[]{:S(2)}) collective-permute-start(bf16[512,256]{1,0:T(8,128)(2,1)S(1)} %get-tuple-element.27.early_ref), channel_id=1, source_target_pairs={{25,16},{29,20},{2,25},{6,29}} | collective-permute-start | bytes 786440 | tf_op jit(solution)/shard_map/ppermute | solution.py:89
  89.9 6.2 %collective-permute-start.22 = (f32[64,128]{1,0:T(8,128)S(1)}, f32[64,128]{1,0:T(8,128)S(1)}, u32[]{:S(2)}, u32[]{:S(2)}) collective-permute-start(f32[64,128]{1,0:T(8,128)S(1)} %add.56), channel_id=1, source_target_pairs={{0,2},{1,3},{2,0},{3,1},{4,6},{5,7},{6,4},{7,5},{8,10},{9,11},{10,... | collective-permute-start | bytes 98312 | tf_op jit(solution)/shard_map/ppermute | solution.py:168
  90.0 14.6 %collective-permute-start.16 = (bf16[256,256]{1,0:T(8,128)(2,1)S(1)}, bf16[256,256]{1,0:T(8,128)(2,1)S(1)}, u32[]{:S(2)}, u32[]{:S(2)}) collective-permute-start(bf16[256,256]{1,0:T(8,128)(2,1)S(1)} %get-tuple-element.39), channel_id=1, source_target_pairs={{25,15},{29,11},{2,20},{6,16},{17,7},{21,3},{10,28},{14,24}} | collective-permute-start | bytes 393224 | tf_op jit(solution)/shard_map/ppermute | solution.py:89
  96.1 9.7 %collective-permute-start.12 = (bf16[256,256]{1,0:T(8,128)(2,1)S(1)}, bf16[256,256]{1,0:T(8,128)(2,1)S(1)}, u32[]{:S(2)}, u32[]{:S(2)}) collective-permute-start(bf16[256,256]{1,0:T(8,128)(2,1)S(1)} %get-tuple-element.36), channel_id=1, source_target_pairs={{8,1},{12,5},{1,8},{5,12},{17,10},{21,14},{10,17},{14,21},{26,19},... | collective-permute-start | bytes 393224 | tf_op jit(solution)/shard_map/ppermute | solution.py:89
  98.1 14.0 %collective-permute-start.13 = (bf16[256,256]{1,0:T(8,128)(2,1)S(1)}, bf16[256,256]{1,0:T(8,128)(2,1)S(1)}, u32[]{:S(2)}, u32[]{:S(2)}) collective-permute-start(bf16[256,256]{1,0:T(8,128)(2,1)S(1)} %get-tuple-element.37), channel_id=1, source_target_pairs={{8,5},{12,1},{1,12},{5,8},{17,14},{21,10},{10,21},{14,17},{26,23},... | collective-permute-start | bytes 393224 | tf_op jit(solution)/shard_map/ppermute | solution.py:89

commit v2 on v1

v2 whole, which is shorter than its diff:
```python
import jax
import jax.numpy as jnp
from jax import lax
from jax.experimental import pallas as pl
from jax.experimental.pallas import tpu as pltpu
from jax.sharding import PartitionSpec as P


VMEM_LIMIT = 18 * 2**20


def general_plan(coef, half_ints, metric_inv, dom_blocks, dom_len):
    lmo_count, domain, ao_rows = half_ints.shape
    block = metric_inv.shape[1]
    slots = domain // block
    fit_blocks = metric_inv.shape[0]
    metric_rows = metric_inv[dom_blocks]
    raw_ints = half_ints.reshape(lmo_count, slots, block, ao_rows)
    fitted = jnp.einsum(
        "isab,isbm->isam", metric_rows, raw_ints, preferred_element_type=jnp.float32
    )
    live_slots = jnp.arange(slots, dtype=jnp.int32)[None, :] < dom_len[:, None]
    fitted = jnp.where(live_slots[:, :, None, None], fitted, 0.0)
    fitted = fitted.reshape(lmo_count, domain, ao_rows).astype(jnp.bfloat16)
    pair_part = jnp.einsum("ipm,mi->ip", fitted, coef, preferred_element_type=jnp.float32)
    one_hot = (
        dom_blocks[:, :, None] == jnp.arange(fit_blocks, dtype=jnp.int32)[None, None, :]
    ).astype(jnp.float32)
    local_density = jnp.einsum("isf,isr->fr", one_hot, pair_part.reshape(lmo_count, slots, block))
    density = lax.psum(local_density, ("occ", "ao"))
    density = density.reshape(fit_blocks * block)
    partial_value = jnp.einsum(
        "ipm,ipn->mn",
        fitted,
        lax.all_gather(fitted, "ao", axis=2, tiled=True),
        preferred_element_type=jnp.float32,
    )
    exchange_k = lax.psum_scatter(partial_value, "occ", scatter_dimension=1, tiled=True)
    return (exchange_k, density)


def line_plan(n_occ, n_ao):
    chips = n_occ // 2

    def device(chip, core, plane):
        return (2 * chip + core) * n_ao + plane

    def both_cores(moves, swap=0):
        return [
            (device(src[1], core, src[0]), device(dst[1], core ^ swap, dst[0]))
            for src, dst in moves
            for core in range(2)
        ]

    def one_core(moves):
        return [
            (device(chip, core, src), device(chip, core, dst))
            for core, src, dst in moves
            for chip in range(chips)
        ]

    spots = [(p, c) for p in range(n_ao) for c in range(chips)]

    far_turn = [((1, 3), (3, 1)), ((2, 0), (0, 2))]
    near_turn = [((p, c), (c, p)) for p, c in spots if abs(p - c) == 1]
    near_turn += [((1, 3), (2, 0)), ((2, 0), (3, 1)), ((1, 1), (3, 0)), ((2, 2), (0, 3))]
    near_straight = [((1, 3), (0, 2)), ((2, 0), (1, 3)), ((1, 1), (0, 3)), ((2, 2), (3, 0))]

    def on_device(coef, half_ints, metric_inv, dom_blocks, dom_len):
        _, domain, ao_rows = half_ints.shape
        fit_blocks, block, _ = metric_inv.shape
        slots = domain // block
        half = ao_rows // 2
        bf16, f32 = jnp.bfloat16, jnp.float32
        plane = lax.axis_index("ao")
        occ = lax.axis_index("occ")
        chip, core = occ // 2, occ % 2
        active = (core + plane) % 2 == 1
        place = jnp.stack([plane, chip, core, active.astype(jnp.int32)]).astype(jnp.int32)
        both = ("occ", "ao")
        whole_vmem = pl.BlockSpec(memory_space=pltpu.VMEM)
        whole_smem = pl.BlockSpec(memory_space=pltpu.SMEM)

        def send(x, pairs):
            return lax.ppermute(x, both, pairs)

        def call(body, inputs, outputs, scratch=(), flops=0, moved=0, far_inputs=0, out_space=None):
            near_inputs = len(inputs) - far_inputs
            return pl.pallas_call(
                body,
                out_shape=[jax.ShapeDtypeStruct(s, d) for s, d in outputs],
                in_specs=[whole_smem] + [whole_vmem] * near_inputs + [hbm] * far_inputs,
                out_specs=[out_space or whole_vmem] * len(outputs),
                scratch_shapes=list(scratch),
                cost_estimate=pl.CostEstimate(flops=flops, bytes_accessed=moved, transcendentals=0),
                compiler_params=pltpu.CompilerParams(vmem_limit_bytes=VMEM_LIMIT),
            )(place, *inputs)

        hbm = pl.BlockSpec(memory_space=pl.ANY)
        in_hbm = pl.BlockSpec(memory_space=pltpu.HBM)

        def group_copies(source, to, sems):
            rows = [pl.ds(g * group, group) for g in range(groups)]
            return [pltpu.make_async_copy(source.at[r, :], to.at[r, :], sems.at[g]) for g, r in enumerate(rows)]

        def fit_in_place(metric_ref, ints_ref, copies, turned_ref=None):
            for g, copy in enumerate(copies):
                copy.wait()
                rows = slice(g * group, (g + 1) * group)
                value = jnp.dot(metric_ref[g], ints_ref[rows, :], preferred_element_type=f32).astype(bf16)
                ints_ref[rows, :] = value
                if turned_ref is not None:
                    turned_ref[:, rows] = value.T

        def put_halves(at, stage_ref, own_hbm, give_hbm, j, sems, act):
            for h in range(2):
                part = stage_ref.at[j, :, pl.ds(h * half, half)]

                @pl.when(at[2] == h)
                def _():
                    act(pltpu.make_async_copy(part, own_hbm.at[j], sems.at[j, h]))

                @pl.when(at[2] != h)
                def _():
                    act(pltpu.make_async_copy(part, give_hbm.at[j], sems.at[j, h]))

        def start(copy):
            copy.start()

        def wait(copy):
            copy.wait()

        def product(turned_ref, right_ref):
            return jnp.dot(turned_ref[...], right_ref[...], preferred_element_type=f32).astype(bf16)

        raw = half_ints[0]
        low = send(raw, one_core([(0, 0, 1), (0, 2, 3), (1, 1, 2)]))
        high = send(raw, one_core([(0, 2, 1), (1, 1, 0), (1, 3, 2)]))
        far = send(raw, one_core([(0, 3, 1), (1, 0, 2)]))

        live = jnp.arange(slots, dtype=jnp.int32) < dom_len[0]
        metric = jnp.where(live[:, None, None], metric_inv[dom_blocks[0]], 0)
        wide = 2 if slots % 2 == 0 else 1
        groups, group = slots // wide, wide * block
        on_diagonal = jnp.eye(wide, dtype=bool)[None, :, None, :, None]
        metric_wide = jnp.where(
            on_diagonal, metric.reshape(groups, wide, block, 1, block), jnp.zeros((), bf16)
        ).reshape(groups, group, group)
        piece = (ao_rows, half)
        fitted = (domain, ao_rows)
        product_flops = 2 * domain * ao_rows * ao_rows

        def own_body(at, metric_ref, coef_ref, raw_hbm, turned_ref, keep_ref, give_ref, pair_ref, mine_ref, sems):
            copies = group_copies(raw_hbm, mine_ref, sems)
            for copy in copies:
                copy.start()
            fit_in_place(metric_ref, mine_ref, copies, turned_ref)
            value = jnp.dot(turned_ref[...], mine_ref[...], preferred_element_type=f32)
            for h in range(2):
                part = value[:, h * half : (h + 1) * half]

                @pl.when(at[2] == h)
                def _():
                    keep_ref[...] = part

                @pl.when(at[2] != h)
                def _():
                    give_ref[...] = part.astype(bf16)

            pair_ref[...] = jnp.dot(coef_ref[...], turned_ref[...], preferred_element_type=f32)

        lines = 16
        mine_turned, square_keep, square_give, pair = call(
            own_body,
            [metric_wide, jnp.broadcast_to(coef.T, (lines, ao_rows)), raw],
            [(fitted[::-1], bf16), (piece, f32), (piece, bf16), ((lines, domain), f32)],
            [pltpu.VMEM(fitted, bf16), pltpu.SemaphoreType.DMA((groups,))],
            product_flops,
            4 * 2**20,
            far_inputs=1,
        )
        swap = [(i, i ^ 1) for i in range(n_occ)]
        square_got = lax.ppermute(square_give, "occ", swap)
        one_hot = dom_blocks[0][:, None] == jnp.arange(fit_blocks, dtype=jnp.int32)
        density = jnp.einsum(
            "sf,sr->fr",
            one_hot.astype(f32),
            pair[0].reshape(slots, block),
            precision=lax.Precision.HIGHEST,
        )
        for axis, n, bit in (("occ", n_occ, 1), ("occ", n_occ, 2), ("occ", n_occ, 4), ("ao", n_ao, 1), ("ao", n_ao, 2)):
            density = density + lax.ppermute(density, axis, [(i, i ^ bit) for i in range(n)])

        square_tile = (ao_rows, ao_rows)

        def far_body(
            at, metric_ref, turned_ref, far_hbm,
            own_hbm, give_hbm, fit_hbm,
            far_ref, stage, in_sems, out_sems, fit_sem,
        ):
            copies = group_copies(far_hbm, far_ref, in_sems)

            @pl.when((at[3] == 1) & (at[0] >= 1) & (at[0] <= n_ao - 2))
            def _():
                for copy in copies:
                    copy.start()
                fit_in_place(metric_ref, far_ref, copies)
                fit_out = pltpu.make_async_copy(far_ref, fit_hbm, fit_sem)
                fit_out.start()
                stage[0] = product(turned_ref, far_ref)
                put_halves(at, stage, own_hbm, give_hbm, 0, out_sems, start)
                fit_out.wait()
                put_halves(at, stage, own_hbm, give_hbm, 0, out_sems, wait)

        far_own, far_give, far_fit = call(
            far_body,
            [metric_wide, mine_turned, far],
            [((1, *piece), bf16), ((1, *piece), bf16), (fitted, bf16)],
            [
                pltpu.VMEM(fitted, bf16),
                pltpu.VMEM((1, *square_tile), bf16),
                pltpu.SemaphoreType.DMA((groups,)),
                pltpu.SemaphoreType.DMA((1, 2)),
                pltpu.SemaphoreType.DMA,
            ],
            product_flops,
            4 * 2**20,
            far_inputs=1,
            out_space=in_hbm,
        )
        far_got = lax.ppermute(far_give, "occ", swap)

        def exchange(pieces):
            parts = [pieces[0]]
            for k in range(1, chips):
                parts.append(lax.ppermute(pieces[k], "occ", [(i, i ^ (2 * k)) for i in range(n_occ)]))
            return parts

        def pick(own_all, got_all, index_of, square_parts=()):
            count = own_all.shape[0]

            def body(at, *refs):
                parts, (own_hbm, got_hbm), rest = refs[: len(square_parts)], refs[len(square_parts) :][:2], refs[len(square_parts) + 2 :]
                outs, sems = rest[:chips], rest[chips]
                busy = at[3] == 1
                steps = []
                for k in range(chips):
                    j = index_of(at[0], at[1] ^ k)
                    safe = jnp.clip(j, 0, count - 1)
                    from_own = pltpu.make_async_copy(own_hbm.at[safe], outs[k], sems.at[k])
                    from_got = pltpu.make_async_copy(got_hbm.at[safe], outs[k], sems.at[k])
                    steps.append((j, from_own, from_got))

                    @pl.when((j >= 0) & busy)
                    def _():
                        from_own.start()

                    @pl.when((j >= 0) & jnp.logical_not(busy))
                    def _():
                        from_got.start()

                for k, (j, from_own, _) in enumerate(steps):
                    if parts:

                        @pl.when(j < 0)
                        def _():
                            outs[k][...] = (parts[0][...] + parts[1][...].astype(f32)).astype(bf16)

                    @pl.when(j >= 0)
                    def _():
                        from_own.wait()

            return call(
                body,
                [*square_parts, own_all, got_all],
                [(piece, bf16)] * chips,
                [pltpu.SemaphoreType.DMA((chips,))],
                0,
                2 * 2**20,
                far_inputs=2,
            )

        def far_index(plane_now, goal):
            return jnp.where(goal == plane_now, -1, 0)

        picked = pick(far_own, far_got, far_index, (square_keep, square_got))
        far_parts = exchange(picked)

        def sum_body(at, a_ref, b_ref, c_ref, d_ref, total_ref, same_ref, other_ref, full):
            core_now = at[2]
            full[...] = (
                a_ref[...].astype(f32) + b_ref[...].astype(f32) + c_ref[...].astype(f32) + d_ref[...].astype(f32)
            )
            total_ref[...] = full[...].astype(bf16)
            for h in range(2):
                turned = full[h * half : (h + 1) * half, :].T.astype(bf16)

                @pl.when(core_now == h)
                def _():
                    same_ref[...] = turned

                @pl.when(core_now != h)
                def _():
                    other_ref[...] = turned

        corner = (half, half)

        def sum_up(parts):
            return call(
                sum_body, parts, [(piece, bf16), (corner, bf16), (corner, bf16)], [pltpu.VMEM(piece, f32)], 0, 2 * 2**20
            )

        far_total, far_same, far_other = sum_up(far_parts)

        def near_body(
            at, metric_ref, turned_hbm, low_hbm, high_hbm, fit_hbm,
            own_hbm, give_hbm,
            low_ref, high_ref, far_ref, low_turned, high_turned, turned_ref, stage, in_sems, out_sems, more_sems,
        ):
            plane_now, busy = at[0], at[3] == 1
            has_low, has_high = busy & (plane_now >= 1), busy & (plane_now <= n_ao - 2)
            inner = has_low & has_high
            low_copies = group_copies(low_hbm, low_ref, in_sems.at[0])
            high_copies = group_copies(high_hbm, high_ref, in_sems.at[1])
            turned_copy = pltpu.make_async_copy(turned_hbm, turned_ref, more_sems.at[0])
            far_copy = pltpu.make_async_copy(fit_hbm, far_ref, more_sems.at[1])

            @pl.when(has_low)
            def _():
                for copy in low_copies:
                    copy.start()

            @pl.when(busy)
            def _():
                turned_copy.start()

            @pl.when(has_high)
            def _():
                for copy in high_copies:
                    copy.start()

            @pl.when(inner)
            def _():
                far_copy.start()

            @pl.when(has_low)
            def _():
                fit_in_place(metric_ref, low_ref, low_copies, low_turned)

            @pl.when(busy)
            def _():
                turned_copy.wait()

            @pl.when(has_low)
            def _():
                stage[0] = product(turned_ref, low_ref)
                put_halves(at, stage, own_hbm, give_hbm, 0, out_sems, start)

            @pl.when(has_high)
            def _():
                fit_in_place(metric_ref, high_ref, high_copies, high_turned)
                stage[1] = product(turned_ref, high_ref)
                put_halves(at, stage, own_hbm, give_hbm, 1, out_sems, start)

            @pl.when(inner)
            def _():
                stage[2] = product(low_turned, high_ref)
                put_halves(at, stage, own_hbm, give_hbm, 2, out_sems, start)
                far_copy.wait()

                @pl.when(plane_now == 1)
                def _():
                    stage[3] = product(low_turned, far_ref)

                @pl.when(plane_now != 1)
                def _():
                    stage[3] = product(high_turned, far_ref)

                put_halves(at, stage, own_hbm, give_hbm, 3, out_sems, start)

            @pl.when(has_low)
            def _():
                put_halves(at, stage, own_hbm, give_hbm, 0, out_sems, wait)

            @pl.when(has_high)
            def _():
                put_halves(at, stage, own_hbm, give_hbm, 1, out_sems, wait)

            @pl.when(inner)
            def _():
                put_halves(at, stage, own_hbm, give_hbm, 2, out_sems, wait)
                put_halves(at, stage, own_hbm, give_hbm, 3, out_sems, wait)

        near_own, near_give = call(
            near_body,
            [metric_wide, mine_turned, low, high, far_fit],
            [((4, *piece), bf16), ((4, *piece), bf16)],
            [
                pltpu.VMEM(fitted, bf16),
                pltpu.VMEM(fitted, bf16),
                pltpu.VMEM(fitted, bf16),
                pltpu.VMEM(fitted[::-1], bf16),
                pltpu.VMEM(fitted[::-1], bf16),
                pltpu.VMEM(fitted[::-1], bf16),
                pltpu.VMEM((4, *square_tile), bf16),
                pltpu.SemaphoreType.DMA((2, groups)),
                pltpu.SemaphoreType.DMA((4, 2)),
                pltpu.SemaphoreType.DMA((2,)),
            ],
            4 * product_flops,
            8 * 2**20,
            far_inputs=4,
            out_space=in_hbm,
        )
        near_got = lax.ppermute(near_give, "occ", swap)

        def near_index(plane_now, goal):
            away = goal - plane_now
            beside = jnp.where(away == -1, 0, 1)
            return jnp.where(jnp.abs(away) == 1, beside, jnp.where(away == 0, 3, 2))

        picked = pick(near_own, near_got, near_index)
        near_total, near_same, near_other = sum_up(exchange(picked))

        arrived = [
            send(near_same, both_cores(near_turn)),
            send(near_other, both_cores(near_turn, 1)),
            send(near_total, both_cores(near_straight)),
            send(far_same, both_cores(far_turn)),
            send(far_other, both_cores(far_turn, 1)),
        ]

        def last_body(at, near_ref, far_ref, ns, no, nd, fs, fo, out_ref):
            plane_now, chip_now, core_now = at[0], at[1], at[2]
            gap = jnp.abs(plane_now - chip_now)
            in_middle = (plane_now >= 1) & (plane_now <= n_ao - 2)
            out_ref[...] = nd[...].astype(f32)

            @pl.when(gap == 1)
            def _():
                out_ref[...] += near_ref[...].astype(f32)

            @pl.when((gap == 0) | ((gap == 2) & in_middle))
            def _():
                out_ref[...] += far_ref[...].astype(f32)

            same_rows = pl.ds(pl.multiple_of(core_now * half, half), half)
            other_rows = pl.ds(pl.multiple_of((1 - core_now) * half, half), half)
            out_ref[same_rows, :] += ns[...].astype(f32) + fs[...].astype(f32)
            out_ref[other_rows, :] += no[...].astype(f32) + fo[...].astype(f32)

        (exchange_k,) = call(last_body, [near_total, far_total, *arrived], [(piece, f32)], [], 0, 3 * 2**20)
        return exchange_k, density.reshape(fit_blocks * block)

    return on_device


def solution(mesh):
    n_occ, n_ao = mesh.shape["occ"], mesh.shape["ao"]
    in_specs = (P("ao", "occ"), P("occ", None, "ao"), P(), P("occ", None), P("occ"))
    out_specs = (P("ao", "occ"), P())

    def sharded(body):
        return jax.shard_map(body, mesh=mesh, in_specs=in_specs, out_specs=out_specs, check_vma=False)

    if not (n_ao == 4 and n_occ == 2 * n_ao):
        return sharded(general_plan)

    def whole(*args):
        if args[1].shape[0] != n_occ:
            return sharded(general_plan)(*args)
        return sharded(line_plan(n_occ, n_ao))(*args)

    return whole
```

time: 114 us -> 95.1 us (0.83)
  the two profiles are of different devices: /device:TPU:13 before, /device:TPU:17 now
where the time goes in v2:
time: 95.1 us; the launch traced here: 94.7 us
  waiting for transfers between devices  42.5 us (45%)
  starting transfers between devices  25.5 us (27%)
  Pallas kernels  16.8 us (18%)
  local copies, waits for them, and re-layouts  5.34 us (6%)
  other arithmetic  2.61 us (3%)
  between operations  1.61 us (2%)
    ppermute x8, waiting for transfers between devices, send(): return lax.ppermute(x, both, pairs)  24.6 us
    pallas_call x8, Pallas kernels, call(): pl.pallas_call(body, out_shape=[jax.ShapeDtypeStruct(s, d) for s, d in ou...  16.8 us
    ppermute x8, starting transfers between devices, send(): return lax.ppermute(x, both, pairs)  15.3 us
    ppermute x5, waiting for transfers between devices, on_device(): lax.ppermute(density, axis, [(i, i ^ bit) for i in range(n)])  10.2 us
    ppermute x6, starting transfers between devices, exchange(): lax.ppermute(pieces[k], 'occ', [(i, i ^ 2 * k) for i in range(n_occ)])  8.45 us
    ppermute x6, waiting for transfers between devices, exchange(): lax.ppermute(pieces[k], 'occ', [(i, i ^ 2 * k) for i in range(n_occ)])  5.64 us
    broadcast_in_dim x3, local copies, waits for them, and re-layouts, on_device(): jnp.where(on_diagonal, metric.reshape(groups, wide, block, 1, block), jnp...  3.46 us
    ppermute x1, waiting for transfers between devices, on_device(): near_got = lax.ppermute(near_give, 'occ', swap)  2.07 us
  transfers between devices with their start and end apart: 22, of which 9 were waited for; matrix products, arithmetic and copies ran while one was open for 7% of the time, Pallas kernels for 9%

profile of v2, /device:TPU:17, one launch (start us, length us, event | category | flops | bytes accessed | tf_op | source)
XLA Modules:
  0.0 94.7 jit_solution(3058162811863981183)
XLA Ops:
  0.7 1.4 %collective-permute-start.2 = (bf16[1024,512]{1,0:T(8,128)(2,1)}, bf16[1024,512]{1,0:T(8,128)(2,1)S(1)}, u32[]{:S(2)}, u32[]{:S(2)}) collective-permute-start(bf16[1024,512]{1,0:T(8,128)(2,1)} %bitcast.22), channel_id=1, source_target_pairs={{3,1},{11,9},{19,17},{27,25},{4,6},{12,14},{20,22},{28,30}} | collective-permute-start | bytes 3145736 | tf_op jit(solution)/shard_map/ppermute | solution.py:85
  2.1 1.3 %collective-permute-start = (bf16[1024,512]{1,0:T(8,128)(2,1)}, bf16[1024,512]{1,0:T(8,128)(2,1)}, u32[]{:S(2)}, u32[]{:S(2)}) collective-permute-start(bf16[1024,512]{1,0:T(8,128)(2,1)} %bitcast.23), channel_id=1, source_target_pairs={{0,1},{8,9},{16,17},{24,25},{2,3},{10,11},{18,19},{26,27},{5,6},{1... | collective-permute-start | bytes 3145736 | tf_op jit(solution)/shard_map/ppermute | solution.py:85
  3.4 1.3 %collective-permute-start.1 = (bf16[1024,512]{1,0:T(8,128)(2,1)}, bf16[1024,512]{1,0:T(8,128)(2,1)}, u32[]{:S(2)}, u32[]{:S(2)}) collective-permute-start(bf16[1024,512]{1,0:T(8,128)(2,1)} %bitcast.24), channel_id=1, source_target_pairs={{2,1},{10,9},{18,17},{26,25},{5,4},{13,12},{21,20},{29,28},{7,6},{... | collective-permute-start | bytes 3145736 | tf_op jit(solution)/shard_map/ppermute | solution.py:85
  4.7 0.7 fusion.2
  6.0 0.6 gather_fusion
  6.6 0.1 broadcast_select_fusion.1
  6.7 1.1 %broadcast_in_dim.54 = bf16[4,2,128,2,128]{4,3,2,1,0:T(2,128)(2,1)} broadcast(bf16[4,2,128,128]{3,2,1,0:T(8,128)(2,1)S(1)} %broadcast_select_fusion.1), dimensions={0,1,2,4} | broadcast | bytes 786432 | tf_op jit(solution)/shard_map/jit(_where)/broadcast_in_dim | solution.py:146
  7.9 2.2 %broadcast_in_dim.55 = bf16[4,256,256]{2,1,0:T(8,128)(2,1)} reshape(bf16[4,2,128,2,128]{4,3,2,1,0:T(2,128)(2,1)} %broadcast_in_dim.54) | data formatting | bytes 1048576 | tf_op jit(solution)/shard_map/jit(_where)/broadcast_in_dim | solution.py:146
  10.1 0.1 broadcast_in_dim.49
  10.3 0.1 pad_add_fusion.at
  10.4 1.1 %broadcast_select_fusion.metric_ref = bf16[4,256,256]{2,1,0:T(8,128)(2,1)S(1)} fusion(bf16[4,256,256]{2,1,0:T(8,128)(2,1)} %broadcast_in_dim.55, pred[256,256]{1,0:T(8,128)(4,1)S(1)} %bitcast.28), kind=kLoop, calls=%fused_computation.1 | loop fusion | flops 262144 | bytes 1114112 | tf_op jit(solution)/shard_map/jit(_where)/select_n | solution.py:146
  11.5 1.2 %copy-done.1 = bf16[1,1024,512]{2,1,0:T(8,128)(2,1)S(1)} copy-done((bf16[1,1024,512]{2,1,0:T(8,128)(2,1)S(1)}, bf16[1,1024,512]{2,1,0:T(8,128)(2,1)}, u32[]{:S(2)}) %copy-start.1) | copy-done | bytes 1048600
  12.7 2.7 %shard_map.68 = (bf16[512,1024]{1,0:T(8,128)(2,1)S(1)}, f32[512,256]{1,0:T(8,128)S(1)}, bf16[512,256]{1,0:T(8,128)(2,1)S(1)}, f32[16,1024]{1,0:T(8,128)S(1)}) custom-call(s32[4]{0:T(128)S(1)} %pad_add_fusion.at, bf16[4,256,256]{2,1,0:T(8,128)(2,1)S(1)} %broadcast_select_fusion.metric_ref, bf16[16,512]{1,0:T(8,128)(2,1)S(1)} %broadcast_in_dim.58.coef_ref, ...), custom_call_target="tpu_custom_call" | custom-call | flops 536870912 | bytes 4194304 | tf_op jit(solution)/shard_map/pallas_call | solution.py:89
  15.4 11.9 %collective-permute-done.2.far_hbm = bf16[1024,512]{1,0:T(8,128)(2,1)S(1)} collective-permute-done((bf16[1024,512]{1,0:T(8,128)(2,1)}, bf16[1024,512]{1,0:T(8,128)(2,1)S(1)}, u32[]{:S(2)}, u32[]{:S(2)}) %collective-permute-start.2) | collective-permute-done | bytes 1048608 | tf_op jit(solution)/shard_map/ppermute | solution.py:85
  27.2 2.5 %shard_map.69 = (bf16[1,512,256]{2,1,0:T(8,128)(2,1)S(1)}, bf16[1,512,256]{2,1,0:T(8,128)(2,1)S(1)}, bf16[1024,512]{1,0:T(8,128)(2,1)S(1)}) custom-call(s32[4]{0:T(128)S(1)} %pad_add_fusion.at, bf16[4,256,256]{2,1,0:T(8,128)(2,1)S(1)} %broadcast_select_fusion.metric_ref, bf16[512,1024]{1,0:T(8,128)(2,1)S(1)} %get-tuple-element.25.turned_ref.turned_hbm, ...), custom_call_target="tpu_custom_call" | custom-call | flops 536870912 | bytes 4194304 | tf_op jit(solution)/shard_map/pallas_call | solution.py:89
  29.7 7.0 %shard_map.70 = (bf16[4,512,256]{2,1,0:T(8,128)(2,1)S(1)}, bf16[4,512,256]{2,1,0:T(8,128)(2,1)S(1)}) custom-call(s32[4]{0:T(128)S(1)} %pad_add_fusion.at, bf16[4,256,256]{2,1,0:T(8,128)(2,1)S(1)} %broadcast_select_fusion.metric_ref, bf16[512,1024]{1,0:T(8,128)(2,1)S(1)} %get-tuple-element.25.turned_ref.turned_hbm, ...), custom_call_target="tpu_custom_call" | custom-call | flops 2147483648 | bytes 8388608 | tf_op jit(solution)/shard_map/pallas_call | solution.py:89
  36.8 0.5 collective-permute-start.7
  37.3 0.1 collective-permute-start.8
  37.4 2.1 %collective-permute-done.3.refs_1_ = bf16[4,512,256]{2,1,0:T(8,128)(2,1)S(1)} collective-permute-done((bf16[4,512,256]{2,1,0:T(8,128)(2,1)S(1)}, bf16[4,512,256]{2,1,0:T(8,128)(2,1)S(1)}, u32[]{:S(2)}, u32[]{:S(2)}) %collective-permute-start.3) | collective-permute-done | bytes 1048608 | tf_op jit(solution)/shard_map/ppermute | solution.py:415
  39.5 0.7 shard_map.71
  40.2 1.3 %collective-permute-start.4 = (bf16[512,256]{1,0:T(8,128)(2,1)S(1)}, bf16[512,256]{1,0:T(8,128)(2,1)S(1)}, u32[]{:S(2)}, u32[]{:S(2)}) collective-permute-start(bf16[512,256]{1,0:T(8,128)(2,1)S(1)} %get-tuple-element.30), channel_id=1, source_target_pairs={{0,8},{4,12},{8,0},{12,4},{16,24},{20,28},{24,16},{28,20},{1,9},{5... | collective-permute-start | bytes 786440 | tf_op jit(solution)/shard_map/ppermute | solution.py:236
  41.5 0.3 fusion
  41.8 0.5 collective-permute-start.17
  42.3 0.9 collective-permute-done.17
  43.1 0.2 collective-permute-start.18
  43.4 1.2 %collective-permute-start.5 = (bf16[512,256]{1,0:T(8,128)(2,1)S(1)}, bf16[512,256]{1,0:T(8,128)(2,1)S(1)}, u32[]{:S(2)}, u32[]{:S(2)}) collective-permute-start(bf16[512,256]{1,0:T(8,128)(2,1)S(1)} %get-tuple-element.31), channel_id=1, source_target_pairs={{0,16},{4,20},{8,24},{12,28},{16,0},{20,4},{24,8},{28,12},{1,17},{... | collective-permute-start | bytes 786440 | tf_op jit(solution)/shard_map/ppermute | solution.py:236
  44.6 4.1 %collective-permute-done.18 = f32[64,128]{1,0:T(8,128)S(1)} collective-permute-done((f32[64,128]{1,0:T(8,128)S(1)}, f32[64,128]{1,0:T(8,128)S(1)}, u32[]{:S(2)}, u32[]{:S(2)}) %collective-permute-start.18) | collective-permute-done | bytes 32800 | tf_op jit(solution)/shard_map/ppermute | solution.py:192
  48.7 2.2 %collective-permute-start.6 = (bf16[512,256]{1,0:T(8,128)(2,1)S(1)}, bf16[512,256]{1,0:T(8,128)(2,1)S(1)}, u32[]{:S(2)}, u32[]{:S(2)}) collective-permute-start(bf16[512,256]{1,0:T(8,128)(2,1)S(1)} %get-tuple-element.32), channel_id=1, source_target_pairs={{0,24},{4,28},{8,16},{12,20},{16,8},{20,12},{24,0},{28,4},{1,25},{... | collective-permute-start | bytes 786440 | tf_op jit(solution)/shard_map/ppermute | solution.py:236
  50.9 0.3 collective-permute-start.19
  51.2 0.8 shard_map.73
  52.0 1.3 %collective-permute-start.10 = (bf16[512,256]{1,0:T(8,128)(2,1)S(1)}, bf16[512,256]{1,0:T(8,128)(2,1)S(1)}, u32[]{:S(2)}, u32[]{:S(2)}) collective-permute-start(bf16[512,256]{1,0:T(8,128)(2,1)S(1)} %get-tuple-element.40), channel_id=1, source_target_pairs={{0,16},{4,20},{8,24},{12,28},{16,0},{20,4},{24,8},{28,12},{1,17},{... | collective-permute-start | bytes 786440 | tf_op jit(solution)/shard_map/ppermute | solution.py:236
  53.3 5.3 %collective-permute-done.19 = f32[64,128]{1,0:T(8,128)S(1)} collective-permute-done((f32[64,128]{1,0:T(8,128)S(1)}, f32[64,128]{1,0:T(8,128)S(1)}, u32[]{:S(2)}, u32[]{:S(2)}) %collective-permute-start.19) | collective-permute-done | bytes 32800 | tf_op jit(solution)/shard_map/ppermute | solution.py:192
  58.6 2.4 %collective-permute-start.9 = (bf16[512,256]{1,0:T(8,128)(2,1)S(1)}, bf16[512,256]{1,0:T(8,128)(2,1)S(1)}, u32[]{:S(2)}, u32[]{:S(2)}) collective-permute-start(bf16[512,256]{1,0:T(8,128)(2,1)S(1)} %get-tuple-element.39), channel_id=1, source_target_pairs={{0,8},{4,12},{8,0},{12,4},{16,24},{20,28},{24,16},{28,20},{1,9},{5... | collective-permute-start | bytes 786440 | tf_op jit(solution)/shard_map/ppermute | solution.py:236
  61.0 0.1 collective-permute-start.20
  61.1 0.8 shard_map.72
  61.9 4.8 %collective-permute-start.14 = (bf16[512,256]{1,0:T(8,128)(2,1)S(1)}, bf16[512,256]{1,0:T(8,128)(2,1)S(1)}, u32[]{:S(2)}, u32[]{:S(2)}) collective-permute-start(bf16[512,256]{1,0:T(8,128)(2,1)S(1)} %get-tuple-element.33.near_ref), channel_id=1, source_target_pairs={{25,16},{29,20},{2,25},{6,29},{9,24},{13,28},{18,3},{22,7}} | collective-permute-start | bytes 786440 | tf_op jit(solution)/shard_map/ppermute | solution.py:85
  66.8 0.1 collective-permute-start.21
  66.9 2.9 %collective-permute-done.10.c_ref = bf16[512,256]{1,0:T(8,128)(2,1)S(1)} collective-permute-done((bf16[512,256]{1,0:T(8,128)(2,1)S(1)}, bf16[512,256]{1,0:T(8,128)(2,1)S(1)}, u32[]{:S(2)}, u32[]{:S(2)}) %collective-permute-start.10) | collective-permute-done | bytes 262176 | tf_op jit(solution)/shard_map/ppermute | solution.py:236
  69.8 2.7 %collective-permute-done.9.b_ref = bf16[512,256]{1,0:T(8,128)(2,1)S(1)} collective-permute-done((bf16[512,256]{1,0:T(8,128)(2,1)S(1)}, bf16[512,256]{1,0:T(8,128)(2,1)S(1)}, u32[]{:S(2)}, u32[]{:S(2)}) %collective-permute-start.9) | collective-permute-done | bytes 262176 | tf_op jit(solution)/shard_map/ppermute | solution.py:236
  72.5 0.8 shard_map.74
  73.3 1.3 %collective-permute-start.15 = (bf16[256,256]{1,0:T(8,128)(2,1)S(1)}, bf16[256,256]{1,0:T(8,128)(2,1)S(1)}, u32[]{:S(2)}, u32[]{:S(2)}) collective-permute-start(bf16[256,256]{1,0:T(8,128)(2,1)S(1)} %get-tuple-element.45), channel_id=1, source_target_pairs={{25,11},{29,15},{2,16},{6,20}} | collective-permute-start | bytes 393224 | tf_op jit(solution)/shard_map/ppermute | solution.py:85
  74.6 1.3 %collective-permute-start.16 = (bf16[256,256]{1,0:T(8,128)(2,1)S(1)}, bf16[256,256]{1,0:T(8,128)(2,1)S(1)}, u32[]{:S(2)}, u32[]{:S(2)}) collective-permute-start(bf16[256,256]{1,0:T(8,128)(2,1)S(1)} %get-tuple-element.46), channel_id=1, source_target_pairs={{25,15},{29,11},{2,20},{6,16}} | collective-permute-start | bytes 393224 | tf_op jit(solution)/shard_map/ppermute | solution.py:85
  75.9 1.9 %collective-permute-start.12 = (bf16[256,256]{1,0:T(8,128)(2,1)S(1)}, bf16[256,256]{1,0:T(8,128)(2,1)S(1)}, u32[]{:S(2)}, u32[]{:S(2)}) collective-permute-start(bf16[256,256]{1,0:T(8,128)(2,1)S(1)} %get-tuple-element.43), channel_id=1, source_target_pairs={{8,1},{12,5},{1,8},{5,12},{17,10},{21,14},{10,17},{14,21},{26,19},... | collective-permute-start | bytes 393224 | tf_op jit(solution)/shard_map/ppermute | solution.py:85
  77.9 1.9 %collective-permute-start.13 = (bf16[256,256]{1,0:T(8,128)(2,1)S(1)}, bf16[256,256]{1,0:T(8,128)(2,1)S(1)}, u32[]{:S(2)}, u32[]{:S(2)}) collective-permute-start(bf16[256,256]{1,0:T(8,128)(2,1)S(1)} %get-tuple-element.44), channel_id=1, source_target_pairs={{8,5},{12,1},{1,12},{5,8},{17,14},{21,10},{10,21},{14,17},{26,23},... | collective-permute-start | bytes 393224 | tf_op jit(solution)/shard_map/ppermute | solution.py:85
  79.8 0.6 add_bitcast_fusion
  80.4 9.1 %collective-permute-done.12.ns = bf16[256,256]{1,0:T(8,128)(2,1)S(1)} collective-permute-done((bf16[256,256]{1,0:T(8,128)(2,1)S(1)}, bf16[256,256]{1,0:T(8,128)(2,1)S(1)}, u32[]{:S(2)}, u32[]{:S(2)}) %collective-permute-start.12) | collective-permute-done | bytes 131104 | tf_op jit(solution)/shard_map/ppermute | solution.py:85
  89.6 3.6 %collective-permute-done.13.no = bf16[256,256]{1,0:T(8,128)(2,1)S(1)} collective-permute-done((bf16[256,256]{1,0:T(8,128)(2,1)S(1)}, bf16[256,256]{1,0:T(8,128)(2,1)S(1)}, u32[]{:S(2)}, u32[]{:S(2)}) %collective-permute-start.13) | collective-permute-done | bytes 131104 | tf_op jit(solution)/shard_map/ppermute | solution.py:85
  93.2 1.6 %shard_map.75 = f32[512,256]{1,0:T(8,128)} custom-call(s32[4]{0:T(128)S(1)} %pad_add_fusion.at, bf16[512,256]{1,0:T(8,128)(2,1)S(1)} %get-tuple-element.33.near_ref, bf16[512,256]{1,0:T(8,128)(2,1)S(1)} %get-tuple-element.42.far_ref, bf16[256,256]{1,0:T(8,128)(2,1)S(1)} %collective-permute-done.12.ns, bf16[256,256]{1,0:T(8,128)(2,1)S(1)} %collective-permute-done.13.no, ...), custom_call_target="tpu_custom_call" | custom-call | bytes 3145728 | tf_op jit(solution)/shard_map/pallas_call | solution.py:89
  (33 shorter events, 0.3 us)
Async XLA Ops:
  0.6 5.4 %copy-start = (bf16[64,128,128]{2,1,0:T(8,128)(2,1)S(1)}, bf16[64,128,128]{2,1,0:T(8,128)(2,1)}, u32[]{:S(2)}) copy-start(bf16[64,128,128]{2,1,0:T(8,128)(2,1)} %param.7) | copy-start | bytes 6291460
  0.6 9.6 %copy-start.2 = (bf16[512,1]{0,1:T(2,128)(2,1)S(1)}, bf16[512,1]{0,1:T(2,128)(2,1)}, u32[]{:S(2)}) copy-start(bf16[512,1]{0,1:T(2,128)(2,1)} %param.5) | copy-start | bytes 3076
  0.7 26.6 %collective-permute-start.2 = (bf16[1024,512]{1,0:T(8,128)(2,1)}, bf16[1024,512]{1,0:T(8,128)(2,1)S(1)}, u32[]{:S(2)}, u32[]{:S(2)}) collective-permute-start(bf16[1024,512]{1,0:T(8,128)(2,1)} %bitcast.22), channel_id=1, source_target_pairs={{3,1},{11,9},{19,17},{27,25},{4,6},{12,14},{20,22},{28,30}} | collective-permute-start | bytes 3145736 | tf_op jit(solution)/shard_map/ppermute | solution.py:85
  2.1 27.6 %collective-permute-start = (bf16[1024,512]{1,0:T(8,128)(2,1)}, bf16[1024,512]{1,0:T(8,128)(2,1)}, u32[]{:S(2)}, u32[]{:S(2)}) collective-permute-start(bf16[1024,512]{1,0:T(8,128)(2,1)} %bitcast.23), channel_id=1, source_target_pairs={{0,1},{8,9},{16,17},{24,25},{2,3},{10,11},{18,19},{26,27},{5,6},{1... | collective-permute-start | bytes 3145736 | tf_op jit(solution)/shard_map/ppermute | solution.py:85
  3.4 26.4 %collective-permute-start.1 = (bf16[1024,512]{1,0:T(8,128)(2,1)}, bf16[1024,512]{1,0:T(8,128)(2,1)}, u32[]{:S(2)}, u32[]{:S(2)}) collective-permute-start(bf16[1024,512]{1,0:T(8,128)(2,1)} %bitcast.24), channel_id=1, source_target_pairs={{2,1},{10,9},{18,17},{26,25},{5,4},{13,12},{21,20},{29,28},{7,6},{... | collective-permute-start | bytes 3145736 | tf_op jit(solution)/shard_map/ppermute | solution.py:85
  11.5 1.2 %copy-start.1 = (bf16[1,1024,512]{2,1,0:T(8,128)(2,1)S(1)}, bf16[1,1024,512]{2,1,0:T(8,128)(2,1)}, u32[]{:S(2)}) copy-start(bf16[1,1024,512]{2,1,0:T(8,128)(2,1)} %param.6) | copy-start | bytes 3145732
  36.8 4.8 %copy-start.3 = (s32[1,8]{1,0:T(1,128)S(1)}, s32[1,8]{1,0:T(1,128)}, u32[]{:S(2)}) copy-start(s32[1,8]{1,0:T(1,128)} %param.8) | copy-start | bytes 100
  36.8 2.7 %collective-permute-start.3 = (bf16[4,512,256]{2,1,0:T(8,128)(2,1)S(1)}, bf16[4,512,256]{2,1,0:T(8,128)(2,1)S(1)}, u32[]{:S(2)}, u32[]{:S(2)}) collective-permute-start(bf16[4,512,256]{2,1,0:T(8,128)(2,1)S(1)} %get-tuple-element.28), channel_id=1, source_target_pairs={{0,4},{4,0},{8,12},{12,8},{16,20},{20,16},{24,28},{28,24},{1,5},{5... | collective-permute-start | bytes 3145736 | tf_op jit(solution)/shard_map/ppermute | solution.py:415
  36.8 14.1 %collective-permute-start.7 = (bf16[512,256]{1,0:T(8,128)(2,1)S(1)}, bf16[512,256]{1,0:T(8,128)(2,1)S(1)}, u32[]{:S(2)}, u32[]{:S(2)}) collective-permute-start(bf16[512,256]{1,0:T(8,128)(2,1)S(1)} %get-tuple-element.35), channel_id=1, source_target_pairs={{0,4},{4,0},{8,12},{12,8},{16,20},{20,16},{24,28},{28,24},{1,5},{5... | collective-permute-start | bytes 786440 | tf_op jit(solution)/shard_map/ppermute | solution.py:183
  37.3 13.9 %collective-permute-start.8 = (bf16[1,512,256]{2,1,0:T(8,128)(2,1)S(1)}, bf16[1,512,256]{2,1,0:T(8,128)(2,1)S(1)}, u32[]{:S(2)}, u32[]{:S(2)}) collective-permute-start(bf16[1,512,256]{2,1,0:T(8,128)(2,1)S(1)} %get-tuple-element.37), channel_id=1, source_target_pairs={{0,4},{4,0},{8,12},{12,8},{16,20},{20,16},{24,28},{28,24},{1,5},{5... | collective-permute-start | bytes 786440 | tf_op jit(solution)/shard_map/ppermute | solution.py:231
  40.2 18.4 %collective-permute-start.4 = (bf16[512,256]{1,0:T(8,128)(2,1)S(1)}, bf16[512,256]{1,0:T(8,128)(2,1)S(1)}, u32[]{:S(2)}, u32[]{:S(2)}) collective-permute-start(bf16[512,256]{1,0:T(8,128)(2,1)S(1)} %get-tuple-element.30), channel_id=1, source_target_pairs={{0,8},{4,12},{8,0},{12,4},{16,24},{20,28},{24,16},{28,20},{1,9},{5... | collective-permute-start | bytes 786440 | tf_op jit(solution)/shard_map/ppermute | solution.py:236
  41.8 1.3 %collective-permute-start.17 = (f32[64,128]{1,0:T(8,128)S(1)}, f32[64,128]{1,0:T(8,128)S(1)}, u32[]{:S(2)}, u32[]{:S(2)}) collective-permute-start(f32[64,128]{1,0:T(8,128)S(1)} %fusion), channel_id=1, source_target_pairs={{0,4},{4,0},{8,12},{12,8},{16,20},{20,16},{24,28},{28,24},{1,5},{5... | collective-permute-start | bytes 98312 | tf_op jit(solution)/shard_map/ppermute | solution.py:192
  43.1 5.6 %collective-permute-start.18 = (f32[64,128]{1,0:T(8,128)S(1)}, f32[64,128]{1,0:T(8,128)S(1)}, u32[]{:S(2)}, u32[]{:S(2)}) collective-permute-start(f32[64,128]{1,0:T(8,128)S(1)} %add.41), channel_id=1, source_target_pairs={{0,8},{4,12},{8,0},{12,4},{16,24},{20,28},{24,16},{28,20},{1,9},{5... | collective-permute-start | bytes 98312 | tf_op jit(solution)/shard_map/ppermute | solution.py:192
  43.4 17.6 %collective-permute-start.5 = (bf16[512,256]{1,0:T(8,128)(2,1)S(1)}, bf16[512,256]{1,0:T(8,128)(2,1)S(1)}, u32[]{:S(2)}, u32[]{:S(2)}) collective-permute-start(bf16[512,256]{1,0:T(8,128)(2,1)S(1)} %get-tuple-element.31), channel_id=1, source_target_pairs={{0,16},{4,20},{8,24},{12,28},{16,0},{20,4},{24,8},{28,12},{1,17},{... | collective-permute-start | bytes 786440 | tf_op jit(solution)/shard_map/ppermute | solution.py:236
  48.7 12.4 %collective-permute-start.6 = (bf16[512,256]{1,0:T(8,128)(2,1)S(1)}, bf16[512,256]{1,0:T(8,128)(2,1)S(1)}, u32[]{:S(2)}, u32[]{:S(2)}) collective-permute-start(bf16[512,256]{1,0:T(8,128)(2,1)S(1)} %get-tuple-element.32), channel_id=1, source_target_pairs={{0,24},{4,28},{8,16},{12,20},{16,8},{20,12},{24,0},{28,4},{1,25},{... | collective-permute-start | bytes 786440 | tf_op jit(solution)/shard_map/ppermute | solution.py:236
  50.9 7.6 %collective-permute-start.19 = (f32[64,128]{1,0:T(8,128)S(1)}, f32[64,128]{1,0:T(8,128)S(1)}, u32[]{:S(2)}, u32[]{:S(2)}) collective-permute-start(f32[64,128]{1,0:T(8,128)S(1)} %add.42), channel_id=1, source_target_pairs={{0,16},{4,20},{8,24},{12,28},{16,0},{20,4},{24,8},{28,12},{1,17},{... | collective-permute-start | bytes 98312 | tf_op jit(solution)/shard_map/ppermute | solution.py:192
  52.0 17.8 %collective-permute-start.10 = (bf16[512,256]{1,0:T(8,128)(2,1)S(1)}, bf16[512,256]{1,0:T(8,128)(2,1)S(1)}, u32[]{:S(2)}, u32[]{:S(2)}) collective-permute-start(bf16[512,256]{1,0:T(8,128)(2,1)S(1)} %get-tuple-element.40), channel_id=1, source_target_pairs={{0,16},{4,20},{8,24},{12,28},{16,0},{20,4},{24,8},{28,12},{1,17},{... | collective-permute-start | bytes 786440 | tf_op jit(solution)/shard_map/ppermute | solution.py:236
  58.5 11.2 %collective-permute-start.11 = (bf16[512,256]{1,0:T(8,128)(2,1)S(1)}, bf16[512,256]{1,0:T(8,128)(2,1)S(1)}, u32[]{:S(2)}, u32[]{:S(2)}) collective-permute-start(bf16[512,256]{1,0:T(8,128)(2,1)S(1)} %get-tuple-element.41), channel_id=1, source_target_pairs={{0,24},{4,28},{8,16},{12,20},{16,8},{20,12},{24,0},{28,4},{1,25},{... | collective-permute-start | bytes 786440 | tf_op jit(solution)/shard_map/ppermute | solution.py:236
  58.6 13.9 %collective-permute-start.9 = (bf16[512,256]{1,0:T(8,128)(2,1)S(1)}, bf16[512,256]{1,0:T(8,128)(2,1)S(1)}, u32[]{:S(2)}, u32[]{:S(2)}) collective-permute-start(bf16[512,256]{1,0:T(8,128)(2,1)S(1)} %get-tuple-element.39), channel_id=1, source_target_pairs={{0,8},{4,12},{8,0},{12,4},{16,24},{20,28},{24,16},{28,20},{1,9},{5... | collective-permute-start | bytes 786440 | tf_op jit(solution)/shard_map/ppermute | solution.py:236
  61.0 5.8 %collective-permute-start.20 = (f32[64,128]{1,0:T(8,128)S(1)}, f32[64,128]{1,0:T(8,128)S(1)}, u32[]{:S(2)}, u32[]{:S(2)}) collective-permute-start(f32[64,128]{1,0:T(8,128)S(1)} %add.43), channel_id=1, source_target_pairs={{0,1},{1,0},{2,3},{3,2},{4,5},{5,4},{6,7},{7,6},{8,9},{9,8},{10,11... | collective-permute-start | bytes 98312 | tf_op jit(solution)/shard_map/ppermute | solution.py:192
  61.9 31.2 %collective-permute-start.14 = (bf16[512,256]{1,0:T(8,128)(2,1)S(1)}, bf16[512,256]{1,0:T(8,128)(2,1)S(1)}, u32[]{:S(2)}, u32[]{:S(2)}) collective-permute-start(bf16[512,256]{1,0:T(8,128)(2,1)S(1)} %get-tuple-element.33.near_ref), channel_id=1, source_target_pairs={{25,16},{29,20},{2,25},{6,29},{9,24},{13,28},{18,3},{22,7}} | collective-permute-start | bytes 786440 | tf_op jit(solution)/shard_map/ppermute | solution.py:85
  66.8 11.1 %collective-permute-start.21 = (f32[64,128]{1,0:T(8,128)S(1)}, f32[64,128]{1,0:T(8,128)S(1)}, u32[]{:S(2)}, u32[]{:S(2)}) collective-permute-start(f32[64,128]{1,0:T(8,128)S(1)} %add.44), channel_id=1, source_target_pairs={{0,2},{1,3},{2,0},{3,1},{4,6},{5,7},{6,4},{7,5},{8,10},{9,11},{10,... | collective-permute-start | bytes 98312 | tf_op jit(solution)/shard_map/ppermute | solution.py:192
  73.3 7.1 %collective-permute-start.15 = (bf16[256,256]{1,0:T(8,128)(2,1)S(1)}, bf16[256,256]{1,0:T(8,128)(2,1)S(1)}, u32[]{:S(2)}, u32[]{:S(2)}) collective-permute-start(bf16[256,256]{1,0:T(8,128)(2,1)S(1)} %get-tuple-element.45), channel_id=1, source_target_pairs={{25,11},{29,15},{2,16},{6,20}} | collective-permute-start | bytes 393224 | tf_op jit(solution)/shard_map/ppermute | solution.py:85
  74.6 5.8 %collective-permute-start.16 = (bf16[256,256]{1,0:T(8,128)(2,1)S(1)}, bf16[256,256]{1,0:T(8,128)(2,1)S(1)}, u32[]{:S(2)}, u32[]{:S(2)}) collective-permute-start(bf16[256,256]{1,0:T(8,128)(2,1)S(1)} %get-tuple-element.46), channel_id=1, source_target_pairs={{25,15},{29,11},{2,20},{6,16}} | collective-permute-start | bytes 393224 | tf_op jit(solution)/shard_map/ppermute | solution.py:85
  75.9 13.6 %collective-permute-start.12 = (bf16[256,256]{1,0:T(8,128)(2,1)S(1)}, bf16[256,256]{1,0:T(8,128)(2,1)S(1)}, u32[]{:S(2)}, u32[]{:S(2)}) collective-permute-start(bf16[256,256]{1,0:T(8,128)(2,1)S(1)} %get-tuple-element.43), channel_id=1, source_target_pairs={{8,1},{12,5},{1,8},{5,12},{17,10},{21,14},{10,17},{14,21},{26,19},... | collective-permute-start | bytes 393224 | tf_op jit(solution)/shard_map/ppermute | solution.py:85
  77.9 15.3 %collective-permute-start.13 = (bf16[256,256]{1,0:T(8,128)(2,1)S(1)}, bf16[256,256]{1,0:T(8,128)(2,1)S(1)}, u32[]{:S(2)}, u32[]{:S(2)}) collective-permute-start(bf16[256,256]{1,0:T(8,128)(2,1)S(1)} %get-tuple-element.44), channel_id=1, source_target_pairs={{8,5},{12,1},{1,12},{5,8},{17,14},{21,10},{10,21},{14,17},{26,23},... | collective-permute-start | bytes 393224 | tf_op jit(solution)/shard_map/ppermute | solution.py:85

commit v3 on v2

--- a/solution.py
+++ b/solution.py
@@ -45,9 +45,9 @@
     def device(chip, core, plane):
         return (2 * chip + core) * n_ao + plane
 
-    def both_cores(moves, swap=0):
+    def both_cores(moves):
         return [
-            (device(src[1], core, src[0]), device(dst[1], core ^ swap, dst[0]))
+            (device(src[1], core, src[0]), device(dst[1], core, dst[0]))
             for src, dst in moves
             for core in range(2)
         ]
@@ -62,7 +62,8 @@
     spots = [(p, c) for p in range(n_ao) for c in range(chips)]
 
     far_turn = [((1, 3), (3, 1)), ((2, 0), (0, 2))]
-    near_turn = [((p, c), (c, p)) for p, c in spots if abs(p - c) == 1]
+    copies = {(0, 1): (0, 2), (3, 2): (3, 1)}
+    near_turn = [(copies.get((p, c), (p, c)), (c, p)) for p, c in spots if abs(p - c) == 1]
     near_turn += [((1, 3), (2, 0)), ((2, 0), (3, 1)), ((1, 1), (3, 0)), ((2, 2), (0, 3))]
     near_straight = [((1, 3), (0, 2)), ((2, 0), (1, 3)), ((1, 1), (0, 3)), ((2, 2), (3, 0))]
 
@@ -84,18 +85,20 @@
         def send(x, pairs):
             return lax.ppermute(x, both, pairs)
 
-        def call(body, inputs, outputs, scratch=(), flops=0, moved=0, far_inputs=0, out_space=None):
+        def call(body, inputs, outputs, scratch=(), flops=0, moved=0, far_inputs=0, out_space=None, scalars=(), far_space=None):
             near_inputs = len(inputs) - far_inputs
             return pl.pallas_call(
                 body,
                 out_shape=[jax.ShapeDtypeStruct(s, d) for s, d in outputs],
-                in_specs=[whole_smem] + [whole_vmem] * near_inputs + [hbm] * far_inputs,
-                out_specs=[out_space or whole_vmem] * len(outputs),
+                in_specs=[whole_smem] * (1 + len(scalars)) + [whole_vmem] * near_inputs + [far_space or hbm] * far_inputs,
+                out_specs=out_space or [whole_vmem] * len(outputs),
                 scratch_shapes=list(scratch),
                 cost_estimate=pl.CostEstimate(flops=flops, bytes_accessed=moved, transcendentals=0),
                 compiler_params=pltpu.CompilerParams(vmem_limit_bytes=VMEM_LIMIT),
-            )(place, *inputs)
-
+            )(place, *scalars, *inputs)
+
+        width = 2 if slots % 2 == 0 else 1
+        groups, group = slots // width, width * block
         hbm = pl.BlockSpec(memory_space=pl.ANY)
         in_hbm = pl.BlockSpec(memory_space=pltpu.HBM)
 
@@ -112,6 +115,12 @@
                 if turned_ref is not None:
                     turned_ref[:, rows] = value.T
 
+        def turn(ints_ref, copies, turned_ref):
+            for g, copy in enumerate(copies):
+                copy.wait()
+                rows = slice(g * group, (g + 1) * group)
+                turned_ref[:, rows] = ints_ref[rows, :].T
+
         def put_halves(at, stage_ref, own_hbm, give_hbm, j, sems, act):
             for h in range(2):
                 part = stage_ref.at[j, :, pl.ds(h * half, half)]
@@ -134,27 +143,31 @@
             return jnp.dot(turned_ref[...], right_ref[...], preferred_element_type=f32).astype(bf16)
 
         raw = half_ints[0]
-        low = send(raw, one_core([(0, 0, 1), (0, 2, 3), (1, 1, 2)]))
-        high = send(raw, one_core([(0, 2, 1), (1, 1, 0), (1, 3, 2)]))
         far = send(raw, one_core([(0, 3, 1), (1, 0, 2)]))
 
-        live = jnp.arange(slots, dtype=jnp.int32) < dom_len[0]
-        metric = jnp.where(live[:, None, None], metric_inv[dom_blocks[0]], 0)
-        wide = 2 if slots % 2 == 0 else 1
-        groups, group = slots // wide, wide * block
-        on_diagonal = jnp.eye(wide, dtype=bool)[None, :, None, :, None]
-        metric_wide = jnp.where(
-            on_diagonal, metric.reshape(groups, wide, block, 1, block), jnp.zeros((), bf16)
-        ).reshape(groups, group, group)
         piece = (ao_rows, half)
         fitted = (domain, ao_rows)
         product_flops = 2 * domain * ao_rows * ao_rows
 
-        def own_body(at, metric_ref, coef_ref, raw_hbm, turned_ref, keep_ref, give_ref, pair_ref, mine_ref, sems):
+        def own_body(
+            at, blocks_at, length_at, coef_ref, metric_hbm, raw_hbm,
+            metric_ref, turned_ref, keep_ref, give_ref, pair_ref, mine_hbm,
+            mine_ref, gathered, sems, metric_sems, mine_sem,
+        ):
+            rows = [pltpu.make_async_copy(metric_hbm.at[blocks_at[0, s]], gathered.at[s], metric_sems.at[s]) for s in range(slots)]
+            for copy in rows:
+                copy.start()
             copies = group_copies(raw_hbm, mine_ref, sems)
             for copy in copies:
                 copy.start()
+            metric_ref[...] = jnp.zeros_like(metric_ref)
+            for s, copy in enumerate(rows):
+                copy.wait()
+                part = slice((s % width) * block, (s % width + 1) * block)
+                metric_ref[s // width, part, part] = jnp.where(s < length_at[0], gathered[s], jnp.zeros((), bf16))
             fit_in_place(metric_ref, mine_ref, copies, turned_ref)
+            mine_copy = pltpu.make_async_copy(mine_ref, mine_hbm, mine_sem)
+            mine_copy.start()
             value = jnp.dot(turned_ref[...], mine_ref[...], preferred_element_type=f32)
             for h in range(2):
                 part = value[:, h * half : (h + 1) * half]
@@ -168,17 +181,29 @@
                     give_ref[...] = part.astype(bf16)
 
             pair_ref[...] = jnp.dot(coef_ref[...], turned_ref[...], preferred_element_type=f32)
+            mine_copy.wait()
 
         lines = 16
-        mine_turned, square_keep, square_give, pair = call(
+        metric_wide, mine_turned, square_keep, square_give, pair, mine = call(
             own_body,
-            [metric_wide, jnp.broadcast_to(coef.T, (lines, ao_rows)), raw],
-            [(fitted[::-1], bf16), (piece, f32), (piece, bf16), ((lines, domain), f32)],
-            [pltpu.VMEM(fitted, bf16), pltpu.SemaphoreType.DMA((groups,))],
+            [jnp.broadcast_to(coef.T, (lines, ao_rows)), metric_inv, raw],
+            [((groups, group, group), bf16), (fitted[::-1], bf16), (piece, f32), (piece, bf16), ((lines, domain), f32), (fitted, bf16)],
+            [
+                pltpu.VMEM(fitted, bf16),
+                pltpu.VMEM((slots, block, block), bf16),
+                pltpu.SemaphoreType.DMA((groups,)),
+                pltpu.SemaphoreType.DMA((slots,)),
+                pltpu.SemaphoreType.DMA,
+            ],
             product_flops,
             4 * 2**20,
-            far_inputs=1,
+            far_inputs=2,
+            out_space=[whole_vmem] * 5 + [in_hbm],
+            scalars=(dom_blocks, dom_len),
+            far_space=in_hbm,
         )
+        low = send(mine, one_core([(0, 0, 1), (0, 2, 3), (1, 1, 2)]))
+        high = send(mine, one_core([(0, 2, 1), (1, 1, 0), (1, 3, 2)]))
         swap = [(i, i ^ 1) for i in range(n_occ)]
         square_got = lax.ppermute(square_give, "occ", swap)
         one_hot = dom_blocks[0][:, None] == jnp.arange(fit_blocks, dtype=jnp.int32)
@@ -226,7 +251,7 @@
             product_flops,
             4 * 2**20,
             far_inputs=1,
-            out_space=in_hbm,
+            out_space=[in_hbm] * 3,
         )
         far_got = lax.ppermute(far_give, "occ", swap)
 
@@ -286,7 +311,7 @@
         picked = pick(far_own, far_got, far_index, (square_keep, square_got))
         far_parts = exchange(picked)
 
-        def sum_body(at, a_ref, b_ref, c_ref, d_ref, total_ref, same_ref, other_ref, full):
+        def sum_body(at, a_ref, b_ref, c_ref, d_ref, total_ref, turned_ref, full):
             core_now = at[2]
             full[...] = (
                 a_ref[...].astype(f32) + b_ref[...].astype(f32) + c_ref[...].astype(f32) + d_ref[...].astype(f32)
@@ -297,23 +322,25 @@
 
                 @pl.when(core_now == h)
                 def _():
-                    same_ref[...] = turned
+                    turned_ref[:half, :] = turned
 
                 @pl.when(core_now != h)
                 def _():
-                    other_ref[...] = turned
-
-        corner = (half, half)
+                    turned_ref[half:, :] = turned
 
         def sum_up(parts):
             return call(
-                sum_body, parts, [(piece, bf16), (corner, bf16), (corner, bf16)], [pltpu.VMEM(piece, f32)], 0, 2 * 2**20
+                sum_body, parts, [(piece, bf16), ((2 * half, half), bf16)], [pltpu.VMEM(piece, f32)], 0, 2 * 2**20
             )
 
-        far_total, far_same, far_other = sum_up(far_parts)
+        def send_turned(turned, moves):
+            arrived = send(turned, both_cores(moves))
+            return arrived, lax.ppermute(arrived[half:], "occ", swap)
+
+        far_total, far_turned = sum_up(far_parts)
 
         def near_body(
-            at, metric_ref, turned_hbm, low_hbm, high_hbm, fit_hbm,
+            at, turned_hbm, low_hbm, high_hbm, fit_hbm,
             own_hbm, give_hbm,
             low_ref, high_ref, far_ref, low_turned, high_turned, turned_ref, stage, in_sems, out_sems, more_sems,
         ):
@@ -345,7 +372,7 @@
 
             @pl.when(has_low)
             def _():
-                fit_in_place(metric_ref, low_ref, low_copies, low_turned)
+                turn(low_ref, low_copies, low_turned)
 
             @pl.when(busy)
             def _():
@@ -358,7 +385,7 @@
 
             @pl.when(has_high)
             def _():
-                fit_in_place(metric_ref, high_ref, high_copies, high_turned)
+                turn(high_ref, high_copies, high_turned)
                 stage[1] = product(turned_ref, high_ref)
                 put_halves(at, stage, own_hbm, give_hbm, 1, out_sems, start)
 
@@ -393,7 +420,7 @@
 
         near_own, near_give = call(
             near_body,
-            [metric_wide, mine_turned, low, high, far_fit],
+            [mine_turned, low, high, far_fit],
             [((4, *piece), bf16), ((4, *piece), bf16)],
             [
                 pltpu.VMEM(fitted, bf16),
@@ -410,24 +437,23 @@
             4 * product_flops,
             8 * 2**20,
             far_inputs=4,
-            out_space=in_hbm,
+            out_space=[in_hbm] * 2,
         )
         near_got = lax.ppermute(near_give, "occ", swap)
 
         def near_index(plane_now, goal):
             away = goal - plane_now
-            beside = jnp.where(away == -1, 0, 1)
-            return jnp.where(jnp.abs(away) == 1, beside, jnp.where(away == 0, 3, 2))
+            beside = jnp.where(away < 0, 0, 1)
+            at_end = (plane_now == 0) | (plane_now == n_ao - 1)
+            return jnp.where((jnp.abs(away) == 1) | at_end, beside, jnp.where(away == 0, 3, 2))
 
         picked = pick(near_own, near_got, near_index)
-        near_total, near_same, near_other = sum_up(exchange(picked))
+        near_total, near_turned = sum_up(exchange(picked))
 
         arrived = [
-            send(near_same, both_cores(near_turn)),
-            send(near_other, both_cores(near_turn, 1)),
+            *send_turned(near_turned, near_turn),
             send(near_total, both_cores(near_straight)),
-            send(far_same, both_cores(far_turn)),
-            send(far_other, both_cores(far_turn, 1)),
+            *send_turned(far_turned, far_turn),
         ]
 
         def last_body(at, near_ref, far_ref, ns, no, nd, fs, fo, out_ref):
@@ -446,7 +472,7 @@
 
             same_rows = pl.ds(pl.multiple_of(core_now * half, half), half)
             other_rows = pl.ds(pl.multiple_of((1 - core_now) * half, half), half)
-            out_ref[same_rows, :] += ns[...].astype(f32) + fs[...].astype(f32)
+            out_ref[same_rows, :] += ns[:half, :].astype(f32) + fs[:half, :].astype(f32)
             out_ref[other_rows, :] += no[...].astype(f32) + fo[...].astype(f32)
 
         (exchange_k,) = call(last_body, [near_total, far_total, *arrived], [(piece, f32)], [], 0, 3 * 2**20)

time: 95.1 us -> 97.1 us (1.021)
  the two profiles are of different devices: /device:TPU:17 before, /device:TPU:0 now
where the time goes in v3:
time: 97.1 us; the launch traced here: 96.8 us
  waiting for transfers between devices  49 us (50%)
  starting transfers between devices  31.5 us (32%)
  Pallas kernels  9.61 us (10%)
  local copies, waits for them, and re-layouts  3.5 us (4%)
  between operations  1.51 us (2%)
  other arithmetic  1.42 us (1%)
    ppermute x6, waiting for transfers between devices, exchange(): lax.ppermute(pieces[k], 'occ', [(i, i ^ 2 * k) for i in range(n_occ)])  20 us
    ppermute x5, waiting for transfers between devices, on_device(): lax.ppermute(density, axis, [(i, i ^ bit) for i in range(n)])  14.5 us
    ppermute x6, waiting for transfers between devices, send(): return lax.ppermute(x, both, pairs)  11.9 us
    ppermute x6, starting transfers between devices, send(): return lax.ppermute(x, both, pairs)  9.62 us
    pallas_call x8, Pallas kernels, call(): pl.pallas_call(body, out_shape=[jax.ShapeDtypeStruct(s, d) for s, d in ou...  9.61 us
    ppermute x5, starting transfers between devices, on_device(): lax.ppermute(density, axis, [(i, i ^ bit) for i in range(n)])  9.25 us
    ppermute x6, starting transfers between devices, exchange(): lax.ppermute(pieces[k], 'occ', [(i, i ^ 2 * k) for i in range(n_occ)])  9.08 us
    unnamed x6, local copies, waits for them, and re-layouts  3.47 us
  transfers between devices with their start and end apart: 22, of which 12 were waited for; matrix products, arithmetic and copies ran while one was open for 2% of the time, Pallas kernels for 8%

profile of v3, /device:TPU:0, one launch (start us, length us, event | category | flops | bytes accessed | tf_op | source)
XLA Modules:
  0.0 96.8 jit_solution(9025693388050477235)
XLA Ops:
  0.6 0.7 collective-permute-start.2
  2.0 0.7 reduce
  2.8 0.1 pad_add_fusion.at
  2.8 1.6 %copy-done = bf16[64,128,128]{2,1,0:T(8,128)(2,1)S(1)} copy-done((bf16[64,128,128]{2,1,0:T(8,128)(2,1)S(1)}, bf16[64,128,128]{2,1,0:T(8,128)(2,1)}, u32[]{:S(2)}) %copy-start) | copy-done | bytes 2097176
  4.4 1.2 %copy-done.1 = bf16[1,1024,512]{2,1,0:T(8,128)(2,1)S(1)} copy-done((bf16[1,1024,512]{2,1,0:T(8,128)(2,1)S(1)}, bf16[1,1024,512]{2,1,0:T(8,128)(2,1)}, u32[]{:S(2)}) %copy-start.1) | copy-done | bytes 1048600
  5.7 0.7 copy-done.2
  6.3 3.5 %shard_map.68 = (bf16[4,256,256]{2,1,0:T(8,128)(2,1)S(1)}, bf16[512,1024]{1,0:T(8,128)(2,1)S(1)}, f32[512,256]{1,0:T(8,128)S(1)}, bf16[512,256]{1,0:T(8,128)(2,1...) custom-call(s32[4]{0:T(128)S(1)} %pad_add_fusion.at, s32[1,8]{1,0:T(1,128)S(1)} %copy-done.2, ...), custom_call_target="tpu_custom_call" | custom-call | flops 536870912 | bytes 4194304 | tf_op jit(solution)/shard_map/pallas_call | solution.py:90
  9.8 0.7 collective-permute-start.1
  10.6 6.1 %collective-permute-start = (bf16[1024,512]{1,0:T(8,128)(2,1)S(1)}, bf16[1024,512]{1,0:T(8,128)(2,1)S(1)}, u32[]{:S(2)}, u32[]{:S(2)}) collective-permute-start(bf16[1024,512]{1,0:T(8,128)(2,1)S(1)} %get-tuple-element.26), channel_id=1, source_target_pairs={{0,1},{8,9},{16,17},{24,25},{2,3},{10,11},{18,19},{26,27},{5,6},{1... | collective-permute-start | bytes 3145736 | tf_op jit(solution)/shard_map/ppermute | solution.py:86
  16.7 0.6 shard_map.69
  17.4 11.8 %collective-permute-done.low_hbm = bf16[1024,512]{1,0:T(8,128)(2,1)S(1)} collective-permute-done((bf16[1024,512]{1,0:T(8,128)(2,1)S(1)}, bf16[1024,512]{1,0:T(8,128)(2,1)S(1)}, u32[]{:S(2)}, u32[]{:S(2)}) %collective-permute-start) | collective-permute-done | bytes 1048608 | tf_op jit(solution)/shard_map/ppermute | solution.py:86
  29.2 0.8 shard_map.70
  30.0 2.4 %collective-permute-start.3 = (bf16[4,512,256]{2,1,0:T(8,128)(2,1)S(1)}, bf16[4,512,256]{2,1,0:T(8,128)(2,1)S(1)}, u32[]{:S(2)}, u32[]{:S(2)}) collective-permute-start(bf16[4,512,256]{2,1,0:T(8,128)(2,1)S(1)} %get-tuple-element.30), channel_id=1, source_target_pairs={{0,4},{4,0},{8,12},{12,8},{16,20},{20,16},{24,28},{28,24},{1,5},{5... | collective-permute-start | bytes 3145736 | tf_op jit(solution)/shard_map/ppermute | solution.py:442
  32.4 0.1 collective-permute-start.7
  32.5 0.4 collective-permute-start.8
  32.9 2.2 %collective-permute-done.7.refs_1_ = bf16[512,256]{1,0:T(8,128)(2,1)S(1)} collective-permute-done((bf16[512,256]{1,0:T(8,128)(2,1)S(1)}, bf16[512,256]{1,0:T(8,128)(2,1)S(1)}, u32[]{:S(2)}, u32[]{:S(2)}) %collective-permute-start.7) | collective-permute-done | bytes 262176 | tf_op jit(solution)/shard_map/ppermute | solution.py:208
  35.1 0.4 collective-permute-done.8.refs_3_
  35.5 0.8 shard_map.73
  36.2 1.6 %collective-permute-start.9 = (bf16[512,256]{1,0:T(8,128)(2,1)S(1)}, bf16[512,256]{1,0:T(8,128)(2,1)S(1)}, u32[]{:S(2)}, u32[]{:S(2)}) collective-permute-start(bf16[512,256]{1,0:T(8,128)(2,1)S(1)} %get-tuple-element.41), channel_id=1, source_target_pairs={{0,8},{4,12},{8,0},{12,4},{16,24},{20,28},{24,16},{28,20},{1,9},{5... | collective-permute-start | bytes 786440 | tf_op jit(solution)/shard_map/ppermute | solution.py:261
  37.8 1.5 %collective-permute-start.10 = (bf16[512,256]{1,0:T(8,128)(2,1)S(1)}, bf16[512,256]{1,0:T(8,128)(2,1)S(1)}, u32[]{:S(2)}, u32[]{:S(2)}) collective-permute-start(bf16[512,256]{1,0:T(8,128)(2,1)S(1)} %get-tuple-element.42), channel_id=1, source_target_pairs={{0,16},{4,20},{8,24},{12,28},{16,0},{20,4},{24,8},{28,12},{1,17},{... | collective-permute-start | bytes 786440 | tf_op jit(solution)/shard_map/ppermute | solution.py:261
  39.3 0.5 collective-permute-start.11
  39.8 0.7 shard_map.71
  40.5 1.6 %collective-permute-start.4 = (bf16[512,256]{1,0:T(8,128)(2,1)S(1)}, bf16[512,256]{1,0:T(8,128)(2,1)S(1)}, u32[]{:S(2)}, u32[]{:S(2)}) collective-permute-start(bf16[512,256]{1,0:T(8,128)(2,1)S(1)} %get-tuple-element.32), channel_id=1, source_target_pairs={{0,8},{4,12},{8,0},{12,4},{16,24},{20,28},{24,16},{28,20},{1,9},{5... | collective-permute-start | bytes 786440 | tf_op jit(solution)/shard_map/ppermute | solution.py:261
  42.1 1.5 %collective-permute-start.5 = (bf16[512,256]{1,0:T(8,128)(2,1)S(1)}, bf16[512,256]{1,0:T(8,128)(2,1)S(1)}, u32[]{:S(2)}, u32[]{:S(2)}) collective-permute-start(bf16[512,256]{1,0:T(8,128)(2,1)S(1)} %get-tuple-element.33), channel_id=1, source_target_pairs={{0,16},{4,20},{8,24},{12,28},{16,0},{20,4},{24,8},{28,12},{1,17},{... | collective-permute-start | bytes 786440 | tf_op jit(solution)/shard_map/ppermute | solution.py:261
  43.6 1.9 %collective-permute-done.9.b_ref = bf16[512,256]{1,0:T(8,128)(2,1)S(1)} collective-permute-done((bf16[512,256]{1,0:T(8,128)(2,1)S(1)}, bf16[512,256]{1,0:T(8,128)(2,1)S(1)}, u32[]{:S(2)}, u32[]{:S(2)}) %collective-permute-start.9) | collective-permute-done | bytes 262176 | tf_op jit(solution)/shard_map/ppermute | solution.py:261
  45.5 2.4 %collective-permute-start.6 = (bf16[512,256]{1,0:T(8,128)(2,1)S(1)}, bf16[512,256]{1,0:T(8,128)(2,1)S(1)}, u32[]{:S(2)}, u32[]{:S(2)}) collective-permute-start(bf16[512,256]{1,0:T(8,128)(2,1)S(1)} %get-tuple-element.34), channel_id=1, source_target_pairs={{0,24},{4,28},{8,16},{12,20},{16,8},{20,12},{24,0},{28,4},{1,25},{... | collective-permute-start | bytes 786440 | tf_op jit(solution)/shard_map/ppermute | solution.py:261
  47.9 4.7 %collective-permute-done.10.c_ref = bf16[512,256]{1,0:T(8,128)(2,1)S(1)} collective-permute-done((bf16[512,256]{1,0:T(8,128)(2,1)S(1)}, bf16[512,256]{1,0:T(8,128)(2,1)S(1)}, u32[]{:S(2)}, u32[]{:S(2)}) %collective-permute-start.10) | collective-permute-done | bytes 262176 | tf_op jit(solution)/shard_map/ppermute | solution.py:261
  52.6 0.8 shard_map.74
  53.4 0.7 collective-permute-start.15
  54.1 2.6 %collective-permute-done.4.b_ref = bf16[512,256]{1,0:T(8,128)(2,1)S(1)} collective-permute-done((bf16[512,256]{1,0:T(8,128)(2,1)S(1)}, bf16[512,256]{1,0:T(8,128)(2,1)S(1)}, u32[]{:S(2)}, u32[]{:S(2)}) %collective-permute-start.4) | collective-permute-done | bytes 262176 | tf_op jit(solution)/shard_map/ppermute | solution.py:261
  56.8 10.8 %collective-permute-done.5.c_ref = bf16[512,256]{1,0:T(8,128)(2,1)S(1)} collective-permute-done((bf16[512,256]{1,0:T(8,128)(2,1)S(1)}, bf16[512,256]{1,0:T(8,128)(2,1)S(1)}, u32[]{:S(2)}, u32[]{:S(2)}) %collective-permute-start.5) | collective-permute-done | bytes 262176 | tf_op jit(solution)/shard_map/ppermute | solution.py:261
  67.6 0.8 shard_map.72
  68.4 0.7 collective-permute-start.12
  69.1 0.3 fusion
  69.4 0.1 collective-permute-start.17
  69.5 1.2 %collective-permute-done.17 = f32[64,128]{1,0:T(8,128)S(1)} collective-permute-done((f32[64,128]{1,0:T(8,128)S(1)}, f32[64,128]{1,0:T(8,128)S(1)}, u32[]{:S(2)}, u32[]{:S(2)}) %collective-permute-start.17) | collective-permute-done | bytes 32800 | tf_op jit(solution)/shard_map/ppermute | solution.py:217
  70.7 5.9 %collective-permute-done.18 = f32[64,128]{1,0:T(8,128)S(1)} collective-permute-done((f32[64,128]{1,0:T(8,128)S(1)}, f32[64,128]{1,0:T(8,128)S(1)}, u32[]{:S(2)}, u32[]{:S(2)}) %collective-permute-start.18) | collective-permute-done | bytes 32800 | tf_op jit(solution)/shard_map/ppermute | solution.py:217
  76.6 1.7 %collective-permute-start.19 = (f32[64,128]{1,0:T(8,128)S(1)}, f32[64,128]{1,0:T(8,128)S(1)}, u32[]{:S(2)}, u32[]{:S(2)}) collective-permute-start(f32[64,128]{1,0:T(8,128)S(1)} %add.30), channel_id=1, source_target_pairs={{0,16},{4,20},{8,24},{12,28},{16,0},{20,4},{24,8},{28,12},{1,17},{... | collective-permute-start | bytes 98312 | tf_op jit(solution)/shard_map/ppermute | solution.py:217
  78.3 2.3 %collective-permute-done.19 = f32[64,128]{1,0:T(8,128)S(1)} collective-permute-done((f32[64,128]{1,0:T(8,128)S(1)}, f32[64,128]{1,0:T(8,128)S(1)}, u32[]{:S(2)}, u32[]{:S(2)}) %collective-permute-start.19) | collective-permute-done | bytes 32800 | tf_op jit(solution)/shard_map/ppermute | solution.py:217
  80.5 3.6 %collective-permute-start.20 = (f32[64,128]{1,0:T(8,128)S(1)}, f32[64,128]{1,0:T(8,128)S(1)}, u32[]{:S(2)}, u32[]{:S(2)}) collective-permute-start(f32[64,128]{1,0:T(8,128)S(1)} %add.31), channel_id=1, source_target_pairs={{0,1},{1,0},{2,3},{3,2},{4,5},{5,4},{6,7},{7,6},{8,9},{9,8},{10,11... | collective-permute-start | bytes 98312 | tf_op jit(solution)/shard_map/ppermute | solution.py:217
  84.1 0.7 collective-permute-start.14
  84.8 1.2 %collective-permute-done.20 = f32[64,128]{1,0:T(8,128)S(1)} collective-permute-done((f32[64,128]{1,0:T(8,128)S(1)}, f32[64,128]{1,0:T(8,128)S(1)}, u32[]{:S(2)}, u32[]{:S(2)}) %collective-permute-start.20) | collective-permute-done | bytes 32800 | tf_op jit(solution)/shard_map/ppermute | solution.py:217
  86.0 4.0 %collective-permute-start.21 = (f32[64,128]{1,0:T(8,128)S(1)}, f32[64,128]{1,0:T(8,128)S(1)}, u32[]{:S(2)}, u32[]{:S(2)}) collective-permute-start(f32[64,128]{1,0:T(8,128)S(1)} %add.32), channel_id=1, source_target_pairs={{0,2},{1,3},{2,0},{3,1},{4,6},{5,7},{6,4},{7,5},{8,10},{9,11},{10,... | collective-permute-start | bytes 98312 | tf_op jit(solution)/shard_map/ppermute | solution.py:217
  90.0 0.1 collective-permute-start.16
  90.1 0.6 collective-permute-start.13
  90.6 4.0 %collective-permute-done.21 = f32[64,128]{1,0:T(8,128)S(1)} collective-permute-done((f32[64,128]{1,0:T(8,128)S(1)}, f32[64,128]{1,0:T(8,128)S(1)}, u32[]{:S(2)}, u32[]{:S(2)}) %collective-permute-start.21) | collective-permute-done | bytes 32800 | tf_op jit(solution)/shard_map/ppermute | solution.py:217
  94.6 0.6 add_bitcast_fusion
  95.2 1.5 %shard_map.75 = f32[512,256]{1,0:T(8,128)} custom-call(s32[4]{0:T(128)S(1)} %pad_add_fusion.at, bf16[512,256]{1,0:T(8,128)(2,1)S(1)} %get-tuple-element.35.near_ref, bf16[512,256]{1,0:T(8,128)(2,1)S(1)} %get-tuple-element.44.far_ref, bf16[512,256]{1,0:T(8,128)(2,1)S(1)} %collective-permute-done.12.ns, bf16[256,256]{1,0:T(8,128)(2,1)S(1)} %collective-permute-done.13.no, ...), custom_call_target="tpu_custom_call" | custom-call | bytes 3145728 | tf_op jit(solution)/shard_map/pallas_call | solution.py:90
  (22 shorter events, 0.1 us)
Async XLA Ops:
  0.6 16.1 %collective-permute-start.2 = (bf16[1024,512]{1,0:T(8,128)(2,1)}, bf16[1024,512]{1,0:T(8,128)(2,1)S(1)}, u32[]{:S(2)}, u32[]{:S(2)}) collective-permute-start(bf16[1024,512]{1,0:T(8,128)(2,1)} %bitcast.10), channel_id=1, source_target_pairs={{3,1},{11,9},{19,17},{27,25},{4,6},{12,14},{20,22},{28,30}} | collective-permute-start | bytes 3145736 | tf_op jit(solution)/shard_map/ppermute | solution.py:86
  2.8 1.6 %copy-start = (bf16[64,128,128]{2,1,0:T(8,128)(2,1)S(1)}, bf16[64,128,128]{2,1,0:T(8,128)(2,1)}, u32[]{:S(2)}) copy-start(bf16[64,128,128]{2,1,0:T(8,128)(2,1)} %metric_hbm.1) | copy-start | bytes 6291460
  4.4 1.2 %copy-start.1 = (bf16[1,1024,512]{2,1,0:T(8,128)(2,1)S(1)}, bf16[1,1024,512]{2,1,0:T(8,128)(2,1)}, u32[]{:S(2)}) copy-start(bf16[1,1024,512]{2,1,0:T(8,128)(2,1)} %param.6) | copy-start | bytes 3145732
  5.7 0.7 copy-start.2
  9.8 7.5 %collective-permute-start.1 = (bf16[1024,512]{1,0:T(8,128)(2,1)S(1)}, bf16[1024,512]{1,0:T(8,128)(2,1)S(1)}, u32[]{:S(2)}, u32[]{:S(2)}) collective-permute-start(bf16[1024,512]{1,0:T(8,128)(2,1)S(1)} %get-tuple-element.26), channel_id=1, source_target_pairs={{2,1},{10,9},{18,17},{26,25},{5,4},{13,12},{21,20},{29,28},{7,6},{... | collective-permute-start | bytes 3145736 | tf_op jit(solution)/shard_map/ppermute | solution.py:86
  10.6 18.6 %collective-permute-start = (bf16[1024,512]{1,0:T(8,128)(2,1)S(1)}, bf16[1024,512]{1,0:T(8,128)(2,1)S(1)}, u32[]{:S(2)}, u32[]{:S(2)}) collective-permute-start(bf16[1024,512]{1,0:T(8,128)(2,1)S(1)} %get-tuple-element.26), channel_id=1, source_target_pairs={{0,1},{8,9},{16,17},{24,25},{2,3},{10,11},{18,19},{26,27},{5,6},{1... | collective-permute-start | bytes 3145736 | tf_op jit(solution)/shard_map/ppermute | solution.py:86
  30.0 9.7 %collective-permute-start.3 = (bf16[4,512,256]{2,1,0:T(8,128)(2,1)S(1)}, bf16[4,512,256]{2,1,0:T(8,128)(2,1)S(1)}, u32[]{:S(2)}, u32[]{:S(2)}) collective-permute-start(bf16[4,512,256]{2,1,0:T(8,128)(2,1)S(1)} %get-tuple-element.30), channel_id=1, source_target_pairs={{0,4},{4,0},{8,12},{12,8},{16,20},{20,16},{24,28},{28,24},{1,5},{5... | collective-permute-start | bytes 3145736 | tf_op jit(solution)/shard_map/ppermute | solution.py:442
  32.4 2.7 %collective-permute-start.7 = (bf16[512,256]{1,0:T(8,128)(2,1)S(1)}, bf16[512,256]{1,0:T(8,128)(2,1)S(1)}, u32[]{:S(2)}, u32[]{:S(2)}) collective-permute-start(bf16[512,256]{1,0:T(8,128)(2,1)S(1)} %get-tuple-element.37), channel_id=1, source_target_pairs={{0,4},{4,0},{8,12},{12,8},{16,20},{20,16},{24,28},{28,24},{1,5},{5... | collective-permute-start | bytes 786440 | tf_op jit(solution)/shard_map/ppermute | solution.py:208
  32.5 3.0 %collective-permute-start.8 = (bf16[1,512,256]{2,1,0:T(8,128)(2,1)S(1)}, bf16[1,512,256]{2,1,0:T(8,128)(2,1)S(1)}, u32[]{:S(2)}, u32[]{:S(2)}) collective-permute-start(bf16[1,512,256]{2,1,0:T(8,128)(2,1)S(1)} %get-tuple-element.39), channel_id=1, source_target_pairs={{0,4},{4,0},{8,12},{12,8},{16,20},{20,16},{24,28},{28,24},{1,5},{5... | collective-permute-start | bytes 786440 | tf_op jit(solution)/shard_map/ppermute | solution.py:256
  36.2 9.2 %collective-permute-start.9 = (bf16[512,256]{1,0:T(8,128)(2,1)S(1)}, bf16[512,256]{1,0:T(8,128)(2,1)S(1)}, u32[]{:S(2)}, u32[]{:S(2)}) collective-permute-start(bf16[512,256]{1,0:T(8,128)(2,1)S(1)} %get-tuple-element.41), channel_id=1, source_target_pairs={{0,8},{4,12},{8,0},{12,4},{16,24},{20,28},{24,16},{28,20},{1,9},{5... | collective-permute-start | bytes 786440 | tf_op jit(solution)/shard_map/ppermute | solution.py:261
  37.8 14.8 %collective-permute-start.10 = (bf16[512,256]{1,0:T(8,128)(2,1)S(1)}, bf16[512,256]{1,0:T(8,128)(2,1)S(1)}, u32[]{:S(2)}, u32[]{:S(2)}) collective-permute-start(bf16[512,256]{1,0:T(8,128)(2,1)S(1)} %get-tuple-element.42), channel_id=1, source_target_pairs={{0,16},{4,20},{8,24},{12,28},{16,0},{20,4},{24,8},{28,12},{1,17},{... | collective-permute-start | bytes 786440 | tf_op jit(solution)/shard_map/ppermute | solution.py:261
  39.3 13.3 %collective-permute-start.11 = (bf16[512,256]{1,0:T(8,128)(2,1)S(1)}, bf16[512,256]{1,0:T(8,128)(2,1)S(1)}, u32[]{:S(2)}, u32[]{:S(2)}) collective-permute-start(bf16[512,256]{1,0:T(8,128)(2,1)S(1)} %get-tuple-element.43), channel_id=1, source_target_pairs={{0,24},{4,28},{8,16},{12,20},{16,8},{20,12},{24,0},{28,4},{1,25},{... | collective-permute-start | bytes 786440 | tf_op jit(solution)/shard_map/ppermute | solution.py:261
  40.5 16.2 %collective-permute-start.4 = (bf16[512,256]{1,0:T(8,128)(2,1)S(1)}, bf16[512,256]{1,0:T(8,128)(2,1)S(1)}, u32[]{:S(2)}, u32[]{:S(2)}) collective-permute-start(bf16[512,256]{1,0:T(8,128)(2,1)S(1)} %get-tuple-element.32), channel_id=1, source_target_pairs={{0,8},{4,12},{8,0},{12,4},{16,24},{20,28},{24,16},{28,20},{1,9},{5... | collective-permute-start | bytes 786440 | tf_op jit(solution)/shard_map/ppermute | solution.py:261
  42.1 25.5 %collective-permute-start.5 = (bf16[512,256]{1,0:T(8,128)(2,1)S(1)}, bf16[512,256]{1,0:T(8,128)(2,1)S(1)}, u32[]{:S(2)}, u32[]{:S(2)}) collective-permute-start(bf16[512,256]{1,0:T(8,128)(2,1)S(1)} %get-tuple-element.33), channel_id=1, source_target_pairs={{0,16},{4,20},{8,24},{12,28},{16,0},{20,4},{24,8},{28,12},{1,17},{... | collective-permute-start | bytes 786440 | tf_op jit(solution)/shard_map/ppermute | solution.py:261
  45.5 22.1 %collective-permute-start.6 = (bf16[512,256]{1,0:T(8,128)(2,1)S(1)}, bf16[512,256]{1,0:T(8,128)(2,1)S(1)}, u32[]{:S(2)}, u32[]{:S(2)}) collective-permute-start(bf16[512,256]{1,0:T(8,128)(2,1)S(1)} %get-tuple-element.34), channel_id=1, source_target_pairs={{0,24},{4,28},{8,16},{12,20},{16,8},{20,12},{24,0},{28,4},{1,25},{... | collective-permute-start | bytes 786440 | tf_op jit(solution)/shard_map/ppermute | solution.py:261
  53.4 36.5 %collective-permute-start.15 = (bf16[512,256]{1,0:T(8,128)(2,1)S(1)}, bf16[512,256]{1,0:T(8,128)(2,1)S(1)}, u32[]{:S(2)}, u32[]{:S(2)}) collective-permute-start(bf16[512,256]{1,0:T(8,128)(2,1)S(1)} %get-tuple-element.46), channel_id=1, source_target_pairs={{25,11},{29,15},{2,16},{6,20}} | collective-permute-start | bytes 786440 | tf_op jit(solution)/shard_map/ppermute | solution.py:86
  68.4 21.6 %collective-permute-start.12 = (bf16[512,256]{1,0:T(8,128)(2,1)S(1)}, bf16[512,256]{1,0:T(8,128)(2,1)S(1)}, u32[]{:S(2)}, u32[]{:S(2)}) collective-permute-start(bf16[512,256]{1,0:T(8,128)(2,1)S(1)} %get-tuple-element.45), channel_id=1, source_target_pairs={{16,1},{20,5},{1,8},{5,12},{17,10},{21,14},{10,17},{14,21},{26,19}... | collective-permute-start | bytes 786440 | tf_op jit(solution)/shard_map/ppermute | solution.py:86
  69.4 1.3 %collective-permute-start.17 = (f32[64,128]{1,0:T(8,128)S(1)}, f32[64,128]{1,0:T(8,128)S(1)}, u32[]{:S(2)}, u32[]{:S(2)}) collective-permute-start(f32[64,128]{1,0:T(8,128)S(1)} %fusion), channel_id=1, source_target_pairs={{0,4},{4,0},{8,12},{12,8},{16,20},{20,16},{24,28},{28,24},{1,5},{5... | collective-permute-start | bytes 98312 | tf_op jit(solution)/shard_map/ppermute | solution.py:217
  70.7 5.9 %collective-permute-start.18 = (f32[64,128]{1,0:T(8,128)S(1)}, f32[64,128]{1,0:T(8,128)S(1)}, u32[]{:S(2)}, u32[]{:S(2)}) collective-permute-start(f32[64,128]{1,0:T(8,128)S(1)} %add.29), channel_id=1, source_target_pairs={{0,8},{4,12},{8,0},{12,4},{16,24},{20,28},{24,16},{28,20},{1,9},{5... | collective-permute-start | bytes 98312 | tf_op jit(solution)/shard_map/ppermute | solution.py:217
  76.6 3.9 %collective-permute-start.19 = (f32[64,128]{1,0:T(8,128)S(1)}, f32[64,128]{1,0:T(8,128)S(1)}, u32[]{:S(2)}, u32[]{:S(2)}) collective-permute-start(f32[64,128]{1,0:T(8,128)S(1)} %add.30), channel_id=1, source_target_pairs={{0,16},{4,20},{8,24},{12,28},{16,0},{20,4},{24,8},{28,12},{1,17},{... | collective-permute-start | bytes 98312 | tf_op jit(solution)/shard_map/ppermute | solution.py:217
  80.5 5.4 %collective-permute-start.20 = (f32[64,128]{1,0:T(8,128)S(1)}, f32[64,128]{1,0:T(8,128)S(1)}, u32[]{:S(2)}, u32[]{:S(2)}) collective-permute-start(f32[64,128]{1,0:T(8,128)S(1)} %add.31), channel_id=1, source_target_pairs={{0,1},{1,0},{2,3},{3,2},{4,5},{5,4},{6,7},{7,6},{8,9},{9,8},{10,11... | collective-permute-start | bytes 98312 | tf_op jit(solution)/shard_map/ppermute | solution.py:217
  84.1 11.1 %collective-permute-start.14 = (bf16[512,256]{1,0:T(8,128)(2,1)S(1)}, bf16[512,256]{1,0:T(8,128)(2,1)S(1)}, u32[]{:S(2)}, u32[]{:S(2)}) collective-permute-start(bf16[512,256]{1,0:T(8,128)(2,1)S(1)} %get-tuple-element.35.near_ref), channel_id=1, source_target_pairs={{25,16},{29,20},{2,25},{6,29},{9,24},{13,28},{18,3},{22,7}} | collective-permute-start | bytes 786440 | tf_op jit(solution)/shard_map/ppermute | solution.py:86
  86.0 8.6 %collective-permute-start.21 = (f32[64,128]{1,0:T(8,128)S(1)}, f32[64,128]{1,0:T(8,128)S(1)}, u32[]{:S(2)}, u32[]{:S(2)}) collective-permute-start(f32[64,128]{1,0:T(8,128)S(1)} %add.32), channel_id=1, source_target_pairs={{0,2},{1,3},{2,0},{3,1},{4,6},{5,7},{6,4},{7,5},{8,10},{9,11},{10,... | collective-permute-start | bytes 98312 | tf_op jit(solution)/shard_map/ppermute | solution.py:217
  90.0 5.2 %collective-permute-start.16 = (bf16[256,256]{1,0:T(8,128)(2,1)S(1)}, bf16[256,256]{1,0:T(8,128)(2,1)S(1)}, u32[]{:S(2)}, u32[]{:S(2)}) collective-permute-start(bf16[256,256]{1,0:T(8,128)(2,1)S(1)} %slice.13), channel_id=1, source_target_pairs={{0,4},{4,0},{8,12},{12,8},{16,20},{20,16},{24,28},{28,24},{1,5},{5... | collective-permute-start | bytes 393224 | tf_op jit(solution)/shard_map/ppermute | solution.py:338
  90.1 5.1 %collective-permute-start.13 = (bf16[256,256]{1,0:T(8,128)(2,1)S(1)}, bf16[256,256]{1,0:T(8,128)(2,1)S(1)}, u32[]{:S(2)}, u32[]{:S(2)}) collective-permute-start(bf16[256,256]{1,0:T(8,128)(2,1)S(1)} %slice.12), channel_id=1, source_target_pairs={{0,4},{4,0},{8,12},{12,8},{16,20},{20,16},{24,28},{28,24},{1,5},{5... | collective-permute-start | bytes 393224 | tf_op jit(solution)/shard_map/ppermute | solution.py:338
